TPU v7x, 32 devices: a whole 2x2x4 slice. The times are simulated.
32 devices in a mesh: rows: 8 (over z, x), cols: 4 (over y, core).
Axes of the slice: x: 2, y: 2, z: 4, core: 2. Of those that a mesh axis runs over, the one named last changes fastest.
Arguments:
- cube: float32 [1, 12288, 12288], P(None, 'rows', 'cols'), may hold values from -480 to 480
Outputs:
- scale_one: float32 [1, 12288, 12288], P(None, 'rows', 'cols')
- scale_two: float32 [1, 12288, 12288], P(None, 'rows', 'cols')
- scale_three: float32 [1, 12288, 12288], P(None, 'rows', 'cols')
- smooth: float32 [1, 12288, 12288], P(None, 'rows', 'cols')
- sigmas: float32 [3, 1], replicated
All inputs are finite; a program needn't handle non-finite values.
Results may differ from a plain program's by a relative error of at most 0.0002.
Values sent between devices are 32-bit elements; how exact they have to be, the bound alone decides.
No kernel may reach another device: no remote copies, remote signals or barrier semaphores. Data moves between devices by JAX's collectives and lax.ppermute only.
A program may use at most 192 MiB of HBM per device.

v0:
```python
import jax
import jax.numpy as jnp
from jax import lax
from jax.sharding import PartitionSpec as P

LEVELS = 3


def padded_2(array, sides, width):
    for axis, dim in sides:
        count, length = (lax.axis_size(axis), array.shape[dim])
        up = [(i, (i + 1) % count) for i in range(count - 1)]
        down = [(j, i) for i, j in up]
        last = lax.slice_in_dim(array, length - width, length, axis=dim)
        leading = lax.slice_in_dim(array, 0, width, axis=dim)
        before = lax.ppermute(last, axis, up)
        after = lax.ppermute(leading, axis, down)
        array = jnp.concatenate([before, array, after], axis=dim)
    return array


def filter_dim(x, dim, step):
    length = x.shape[dim]

    def part(lower, upper):
        return lax.slice_in_dim(x, lower, length - upper, axis=dim)

    outer = (part(0, 4 * step) + part(4 * step, 0)) * 0.0625
    inner = (part(step, 3 * step) + part(3 * step, step)) * 0.25
    return outer + inner + part(2 * step, 2 * step) * 0.375


def mirror_edges(padded, dim, width, position, extent):
    length = padded.shape[dim]
    upper_mirror = jnp.flip(lax.slice_in_dim(padded, width + 1, 2 * width + 1, axis=dim), dim)
    lower_mirror = jnp.flip(
        lax.slice_in_dim(padded, length - 2 * width - 1, length - width - 1, axis=dim), dim
    )
    upper_rim = lax.slice_in_dim(padded, 0, width, axis=dim)
    lower_rim = lax.slice_in_dim(padded, length - width, length, axis=dim)
    middle = lax.slice_in_dim(padded, width, length - width, axis=dim)
    upper_rim = jnp.where(position == 0, upper_mirror, upper_rim)
    lower_rim = jnp.where(position == extent - 1, lower_mirror, lower_rim)
    return jnp.concatenate([upper_rim, middle, lower_rim], axis=dim)


def on_device(cube):
    row_pos = lax.axis_index("rows")
    col_pos = lax.axis_index("cols")
    row_count = lax.axis_size("rows")
    col_count = lax.axis_size("cols")
    pixels = float(row_count * col_count * cube.shape[1] * cube.shape[2])
    planes = []
    sigma_rows = []

    def record(plane):
        square = jnp.sum(plane * plane, axis=(1, 2))
        square = lax.psum(square, ("rows", "cols"))
        sigma_rows.append(jnp.sqrt(square / pixels + 1e-06))

    current = cube
    for level in range(LEVELS):
        step = 2**level
        width = 2 * step
        tall = padded_2(current, (("rows", 1),), width)
        tall = mirror_edges(tall, 1, width, row_pos, row_count)
        filtered = filter_dim(tall, 1, step)
        broad = padded_2(filtered, (("cols", 2),), width)
        broad = mirror_edges(broad, 2, width, col_pos, col_count)
        nextsmooth = filter_dim(broad, 2, step)
        plane = current - nextsmooth
        planes.append(plane)
        record(plane)
        current = nextsmooth
    sigmas = jnp.stack(sigma_rows)
    return (planes[0], planes[1], planes[2], current, sigmas)


def solution(mesh):
    in_specs = (P(None, "rows", "cols"),)
    out_specs = (
        P(None, "rows", "cols"),
        P(None, "rows", "cols"),
        P(None, "rows", "cols"),
        P(None, "rows", "cols"),
        P(),
    )
    return jax.shard_map(
        on_device, mesh=mesh, in_specs=in_specs, out_specs=out_specs, check_vma=False
    )
```

profile of v0, /device:TPU:0, one launch (start us, length us, event | category | flops | bytes accessed | tf_op | source)
XLA Modules:
  0.0 546.7 jit_solution(906147334425397631)
XLA Ops:
  0.6 1.1 fusion.56
  1.7 1.3 collective-permute-start.1
  3.0 5.5 %collective-permute-start = (f32[1,2,3072]{2,1,0:T(2,128)S(1)}, f32[1,2,3072]{2,1,0:T(2,128)S(1)}, u32[]{:S(2)}, u32[]{:S(2)}) collective-permute-start(f32[1,2,3072]{2,1,0:T(2,128)S(1)} %get-tuple-element.47), channel_id=1, source_target_pairs={{0,4},{4,8},{8,12},{12,16},{16,20},{20,24},{24,28},{1,5},{5,9},{9,... | collective-permute-start | bytes 73736 | tf_op jit(solution)/shard_map/ppermute | solution.py:16
  8.5 18.6 %copy.23 = f32[1,1536,3072]{1,2,0:T(8,128)} copy(f32[1,1536,3072]{2,1,0:T(8,128)} %param.1) | data formatting | bytes 37748736 | tf_op args[0]
  27.7 0.6 rev.43
  29.5 50.3 %fusion.34 = f32[1,1536,3072]{1,2,0:T(8,128)} fusion(f32[1,1536,3072]{1,2,0:T(8,128)} %copy.23, f32[1,2,3072]{1,2,0:T(8,128)S(1)} %copy.21, f32[1,2,3072]{1,2,0:T(8,128)S(1)} %copy.18), kind=kLoop, calls=%fused_computation.58 | loop fusion | flops 51904512 | bytes 37797888 | tf_op jit(solution)/shard_map/add | solution.py:30
  79.8 0.9 fusion.55
  80.7 1.5 collective-permute-start.2
  82.8 1.3 collective-permute-start.3
  84.1 3.9 collective-permute-done.3
  88.0 50.7 %multiply_reduce_fusion.2 = (f32[]{:T(128)}, f32[1,1536,3072]{1,2,0:T(8,128)}, f32[1,1536,3072]{1,2,0:T(8,128)}) fusion(f32[1,1536,3072]{1,2,0:T(8,128)} %copy.23, f32[1,1536,3072]{1,2,0:T(8,128)} %fusion.34, f32[1,1536,2]{1,2,0:T(2,128)S(1)} %broadcast_select_fusion.10, f32[1,1536,2]{1,2,0:T(2,128)S(1)} %broadcast_select_fusion.11), kind=kLoop, calls=%fused_computation.86 | loop fusion | flops 66060288 | bytes 75522048 | tf_op jit(solution)/shard_map/reduce_sum | solution.py:57
  138.7 6.1 %fusion.54 = (f32[1,4,3072]{1,2,0:T(8,128)}, f32[1,4,3072]{1,2,0:T(8,128)}, f32[1,4,3072]{1,2,0:T(8,128)S(1)}, f32[1,4,3072]{1,2,0:T(8,128)S(1)}) fusion(f32[1,1536,3072]{1,2,0:T(8,128)} %get-tuple-element.20), kind=kLoop, calls=%fused_computation.103 | loop fusion | bytes 393216 | tf_op jit(solution)/shard_map/slice | solution.py:14
  144.8 1.9 copy.26
  146.6 1.3 collective-permute-start.5
  147.9 1.9 copy.24
  149.8 5.1 collective-permute-start.4
  154.9 8.7 %rev.47 = f32[1,4,3072]{1,2,0:T(8,128)} reverse(f32[1,4,3072]{1,2,0:T(8,128)S(1)} %get-tuple-element.41), dimensions={1} | reverse | bytes 98304 | tf_op jit(solution)/shard_map/jit(_flip)/rev | solution.py:36
  163.6 2.1 rev.46
  165.8 1.7 copy.27
  167.4 1.6 broadcast_select_fusion.2
  169.0 1.7 copy.25
  170.8 50.7 %fusion.28 = f32[1,1536,3072]{1,2,0:T(8,128)} fusion(f32[1,1536,3072]{1,2,0:T(8,128)} %get-tuple-element.20, f32[1,4,3072]{1,2,0:T(8,128)S(1)} %broadcast_select_fusion.2, f32[1,4,3072]{1,2,0:T(8,128)S(1)} %broadcast_select_fusion.3), kind=kLoop, calls=%fused_computation.52 | loop fusion | flops 51904512 | bytes 37847040 | tf_op jit(solution)/shard_map/add | solution.py:30
  221.6 0.9 fusion.53
  222.5 4.1 collective-permute-start.6
  227.2 1.3 collective-permute-start.7
  228.5 1.8 collective-permute-done.7
  230.3 50.8 %multiply_reduce_fusion.1 = (f32[]{:T(128)}, f32[1,1536,3072]{1,2,0:T(8,128)}, f32[1,1536,3072]{1,2,0:T(8,128)}) fusion(f32[1,1536,3072]{1,2,0:T(8,128)} %get-tuple-element.20, f32[1,1536,3072]{1,2,0:T(8,128)} %fusion.28, f32[1,1536,4]{1,2,0:T(4,128)S(1)} %broadcast_select_fusion.8, f32[1,1536,4]{1,2,0:T(4,128)S(1)} %broadcast_select_fusion.9), kind=kLoop, calls=%fused_computation.85 | loop fusion | flops 66060288 | bytes 75546624 | tf_op jit(solution)/shard_map/reduce_sum | solution.py:57
  281.1 6.0 %fusion.52 = (f32[1,8,3072]{1,2,0:T(8,128)}, f32[1,8,3072]{1,2,0:T(8,128)}, f32[1,8,3072]{1,2,0:T(8,128)S(1)}, f32[1,8,3072]{1,2,0:T(8,128)S(1)}) fusion(f32[1,1536,3072]{1,2,0:T(8,128)} %get-tuple-element.23), kind=kLoop, calls=%fused_computation.101 | loop fusion | bytes 786432 | tf_op jit(solution)/shard_map/slice | solution.py:14
  287.2 1.8 copy.30
  289.0 1.3 collective-permute-start.9
  290.3 1.8 copy.28
  292.2 6.9 %collective-permute-start.8 = (f32[1,8,3072]{2,1,0:T(8,128)S(1)}, f32[1,8,3072]{2,1,0:T(8,128)S(1)}, u32[]{:S(2)}, u32[]{:S(2)}) collective-permute-start(f32[1,8,3072]{2,1,0:T(8,128)S(1)} %copy.28), channel_id=1, source_target_pairs={{0,4},{4,8},{8,12},{12,16},{16,20},{20,24},{24,28},{1,5},{5,9},{9,... | collective-permute-start | bytes 294920 | tf_op jit(solution)/shard_map/ppermute | solution.py:16
  299.0 8.7 %rev.51 = f32[1,8,3072]{1,2,0:T(8,128)} reverse(f32[1,8,3072]{1,2,0:T(8,128)S(1)} %get-tuple-element.33), dimensions={1} | reverse | bytes 196608 | tf_op jit(solution)/shard_map/jit(_flip)/rev | solution.py:36
  307.8 2.1 rev.50
  309.9 1.6 copy.31
  311.5 1.6 broadcast_select_fusion
  313.1 1.6 copy.29
  314.9 51.1 %fusion.22 = f32[1,1536,3072]{1,2,0:T(8,128)} fusion(f32[1,1536,3072]{1,2,0:T(8,128)} %get-tuple-element.23, f32[1,8,3072]{1,2,0:T(8,128)S(1)} %broadcast_select_fusion, f32[1,8,3072]{1,2,0:T(8,128)S(1)} %broadcast_select_fusion.1), kind=kLoop, calls=%fused_computation.46 | loop fusion | flops 51904512 | bytes 37945344 | tf_op jit(solution)/shard_map/add | solution.py:30
  365.9 1.0 fusion.51
  367.0 4.2 collective-permute-start.10
  371.2 18.6 %copy.32 = f32[1,1536,3072]{2,1,0:T(8,128)} copy(f32[1,1536,3072]{1,2,0:T(8,128)} %get-tuple-element.19) | data formatting | bytes 37748736
  389.8 18.6 %copy.33 = f32[1,1536,3072]{2,1,0:T(8,128)} copy(f32[1,1536,3072]{1,2,0:T(8,128)} %get-tuple-element.22) | data formatting | bytes 37748736
  408.8 1.3 collective-permute-start.11
  410.2 1.8 collective-permute-done.11
  412.0 50.3 %multiply_reduce_fusion = (f32[]{:T(128)}, f32[1,1536,3072]{1,2,0:T(8,128)}, f32[1,1536,3072]{1,2,0:T(8,128)}) fusion(f32[1,1536,3072]{1,2,0:T(8,128)} %get-tuple-element.23, f32[1,1536,3072]{1,2,0:T(8,128)} %fusion.22, f32[1,1536,8]{1,2,0:T(8,128)S(1)} %broadcast_select_fusion.4, f32[1,1536,8]{1,2,0:T(8,128)S(1)} %broadcast_select_fusion.5), kind=kLoop, calls=%fused_computation.84 | loop fusion | flops 66060288 | bytes 75595776 | tf_op jit(solution)/shard_map/reduce_sum | solution.py:57
  462.2 18.6 %copy.34 = f32[1,1536,3072]{2,1,0:T(8,128)} copy(f32[1,1536,3072]{1,2,0:T(8,128)} %get-tuple-element.25) | data formatting | bytes 37748736
  480.9 44.6 %all-reduce = (f32[1]{0:T(128)}, f32[1]{0:T(128)}, f32[1]{0:T(128)}) all-reduce(f32[1]{0:T(128)} %bitcast.4, f32[1]{0:T(128)} %bitcast.2, f32[1]{0:T(128)} %bitcast), channel_id=1, replica_groups=mesh['rows'=8,'cols'=4] {'rows','cols'}, use_global_device_ids=true, to_apply=%region_5.6 | all-reduce | flops 3 | bytes 24 | tf_op jit(solution)/shard_map/psum | solution.py:58
  527.5 18.6 %copy.35 = f32[1,1536,3072]{2,1,0:T(8,128)} copy(f32[1,1536,3072]{1,2,0:T(8,128)} %get-tuple-element.26) | data formatting | bytes 37748736
  (29 shorter events, 4.3 us)
Async XLA Ops:
  1.7 26.6 %collective-permute-start.1 = (f32[1,2,3072]{2,1,0:T(2,128)S(1)}, f32[1,2,3072]{2,1,0:T(2,128)S(1)}, u32[]{:S(2)}, u32[]{:S(2)}) collective-permute-start(f32[1,2,3072]{2,1,0:T(2,128)S(1)} %get-tuple-element.48), channel_id=1, source_target_pairs={{4,0},{8,4},{12,8},{16,12},{20,16},{24,20},{28,24},{5,1},{9,5},{13... | collective-permute-start | bytes 73736 | tf_op jit(solution)/shard_map/ppermute | solution.py:17
  3.0 25.9 %collective-permute-start = (f32[1,2,3072]{2,1,0:T(2,128)S(1)}, f32[1,2,3072]{2,1,0:T(2,128)S(1)}, u32[]{:S(2)}, u32[]{:S(2)}) collective-permute-start(f32[1,2,3072]{2,1,0:T(2,128)S(1)} %get-tuple-element.47), channel_id=1, source_target_pairs={{0,4},{4,8},{8,12},{12,16},{16,20},{20,24},{24,28},{1,5},{5,9},{9,... | collective-permute-start | bytes 73736 | tf_op jit(solution)/shard_map/ppermute | solution.py:16
  80.7 3.4 collective-permute-start.2
  82.8 5.2 collective-permute-start.3
  146.6 19.1 %collective-permute-start.5 = (f32[1,4,3072]{2,1,0:T(4,128)S(1)}, f32[1,4,3072]{2,1,0:T(4,128)S(1)}, u32[]{:S(2)}, u32[]{:S(2)}) collective-permute-start(f32[1,4,3072]{2,1,0:T(4,128)S(1)} %copy.26), channel_id=1, source_target_pairs={{4,0},{8,4},{12,8},{16,12},{20,16},{24,20},{28,24},{5,1},{9,5},{13... | collective-permute-start | bytes 147464 | tf_op jit(solution)/shard_map/ppermute | solution.py:17
  149.8 19.2 %collective-permute-start.4 = (f32[1,4,3072]{2,1,0:T(4,128)S(1)}, f32[1,4,3072]{2,1,0:T(4,128)S(1)}, u32[]{:S(2)}, u32[]{:S(2)}) collective-permute-start(f32[1,4,3072]{2,1,0:T(4,128)S(1)} %copy.24), channel_id=1, source_target_pairs={{0,4},{4,8},{8,12},{12,16},{16,20},{20,24},{24,28},{1,5},{5,9},{9,... | collective-permute-start | bytes 147464 | tf_op jit(solution)/shard_map/ppermute | solution.py:16
  222.5 6.0 %collective-permute-start.6 = (f32[1,1536,4]{1,2,0:T(4,128)S(1)}, f32[1,1536,4]{1,2,0:T(4,128)S(1)}, u32[]{:S(2)}, u32[]{:S(2)}) collective-permute-start(f32[1,1536,4]{1,2,0:T(4,128)S(1)} %get-tuple-element.35), channel_id=1, source_target_pairs={{0,1},{1,2},{2,3},{4,5},{5,6},{6,7},{8,9},{9,10},{10,11},{12,13},{... | collective-permute-start | bytes 73736 | tf_op jit(solution)/shard_map/ppermute | solution.py:16
  227.2 3.1 collective-permute-start.7
  289.0 20.9 %collective-permute-start.9 = (f32[1,8,3072]{2,1,0:T(8,128)S(1)}, f32[1,8,3072]{2,1,0:T(8,128)S(1)}, u32[]{:S(2)}, u32[]{:S(2)}) collective-permute-start(f32[1,8,3072]{2,1,0:T(8,128)S(1)} %copy.30), channel_id=1, source_target_pairs={{4,0},{8,4},{12,8},{16,12},{20,16},{24,20},{28,24},{5,1},{9,5},{13... | collective-permute-start | bytes 294920 | tf_op jit(solution)/shard_map/ppermute | solution.py:17
  292.2 20.9 %collective-permute-start.8 = (f32[1,8,3072]{2,1,0:T(8,128)S(1)}, f32[1,8,3072]{2,1,0:T(8,128)S(1)}, u32[]{:S(2)}, u32[]{:S(2)}) collective-permute-start(f32[1,8,3072]{2,1,0:T(8,128)S(1)} %copy.28), channel_id=1, source_target_pairs={{0,4},{4,8},{8,12},{12,16},{16,20},{20,24},{24,28},{1,5},{5,9},{9,... | collective-permute-start | bytes 294920 | tf_op jit(solution)/shard_map/ppermute | solution.py:16
  367.0 43.2 %collective-permute-start.10 = (f32[1,1536,8]{1,2,0:T(8,128)S(1)}, f32[1,1536,8]{1,2,0:T(8,128)S(1)}, u32[]{:S(2)}, u32[]{:S(2)}) collective-permute-start(f32[1,1536,8]{1,2,0:T(8,128)S(1)} %get-tuple-element.27), channel_id=1, source_target_pairs={{0,1},{1,2},{2,3},{4,5},{5,6},{6,7},{8,9},{9,10},{10,11},{12,13},{... | collective-permute-start | bytes 147464 | tf_op jit(solution)/shard_map/ppermute | solution.py:16
  408.8 3.1 collective-permute-start.11
where the time goes:
time: 549 us; the launch traced here: 547 us
  other arithmetic  308 us (56%)
  local copies, waits for them, and re-layouts  149 us (27%)
  blocking collectives  44.6 us (8%)
  starting transfers between devices  35 us (6%)
  waiting for transfers between devices  7.45 us (1%)
    add x3, other arithmetic, filter_dim(): return outer + inner + part(2 * step, 2 * step) * 0.375  152 us
    reduce_sum x3, other arithmetic, record(): square = jnp.sum(plane * plane, axis=(1, 2))  152 us
    unnamed x5, local copies, waits for them, and re-layouts  93.2 us
    psum x1, blocking collectives, record(): square = lax.psum(square, ('rows', 'cols'))  44.6 us
    ppermute x6, starting transfers between devices, padded_2(): before = lax.ppermute(last, axis, up)  27.2 us
    slice x8, local copies, waits for them, and re-layouts, padded_2(): last = lax.slice_in_dim(array, length - width, length, axis=dim)  19.7 us
    rev x6, local copies, waits for them, and re-layouts, mirror_edges(): jnp.flip(lax.slice_in_dim(padded, length - 2 * width - 1, length - width...  18.8 us
  transfers between devices with their start and end apart: 12, of which 3 were waited for; matrix products, arithmetic and copies ran while one was open for 17% of the time, Pallas kernels for 0%

commit v1 on v0

v1 whole, which is shorter than its diff:
```python
import functools

import jax
import jax.numpy as jnp
from jax import lax
from jax.experimental import pallas as pl
from jax.experimental.pallas import tpu as pltpu
from jax.sharding import PartitionSpec as P

LANES = 128
TILE = 128
REACH = 14
TOP = 24
HEAD = 16
SIDE = 8
LAG = dict(a=0, b=1, c=2, d=2, e=2, f=3)
SKEW = dict(a=0, b=1, c=2, d=4, e=6, f=7)


def five(load, step):
    a, b, c, d, e = (load(k * step) for k in (-2, -1, 0, 1, 2))
    return (a + e) + 4.0 * (b + d) + 6.0 * c


def kernel(x, top, bottom, sides, w1, w2, w3, smooth, squares, xs, y1t, c1t, c1, z, c2, y3t, o1, o2, o3, o4, acc, isem, osem,
           *, rows, strips):
    tiles = (rows + 2 * HEAD + TILE - 1) // TILE
    outs = ((o1, w1, "b"), (o2, w2, "d"), (o3, w3, "f"), (o4, smooth, "f"))

    def in_copies(strip, slot):
        cols = pl.ds(pl.multiple_of(strip * LANES, LANES), LANES)
        return (
            pltpu.make_async_copy(x.at[:, cols], xs.at[slot, pl.ds(TOP, rows), :], isem.at[slot, 0]),
            pltpu.make_async_copy(top.at[:, cols], xs.at[slot, pl.ds(0, TOP), :], isem.at[slot, 1]),
            pltpu.make_async_copy(bottom.at[:, cols], xs.at[slot, pl.ds(TOP + rows, TOP), :], isem.at[slot, 2]),
        )

    def side_copy(side, slot):
        return pltpu.make_async_copy(sides.at[side], xs.at[slot, pl.ds(0, rows + 2 * TOP), :], isem.at[slot, 0])

    def fetch(s, wait):
        slot = lax.rem(s, 5)
        for side, at in ((0, 0), (1, strips + 1)):

            @pl.when(s == at)
            def _():
                c = side_copy(side, slot)
                c.wait() if wait else c.start()

        @pl.when((s >= 1) & (s <= strips))
        def _():
            for c in in_copies(s - 1, slot):
                c.wait() if wait else c.start()

    def out_copy(k, s):
        buf, dst, _ = outs[k]
        slot = lax.rem(s, 3)
        cols = pl.ds(pl.multiple_of((s - 1) * LANES, LANES), LANES)
        return pltpu.make_async_copy(buf.at[slot, pl.ds(HEAD, rows), :], dst.at[:, cols], osem.at[k, slot])

    def boundary(big):
        fetch(big, True)
        fetch(big + 2, False)
        for k, (_, _, st) in enumerate(outs):
            done = big - LAG[st] - 2

            @pl.when((done - 1 >= 1) & (done - 1 <= strips))
            def _():
                out_copy(k, done - 1).wait()

            @pl.when((done >= 1) & (done <= strips))
            def _():
                out_copy(k, done).start()

    def place(st, big, r):
        q = r - SKEW[st]
        behind = q < 0
        rb = jnp.where(behind, q + tiles, q)
        s = big - LAG[st] - jnp.where(behind, 1, 0)
        return s, rb

    def ring(s, n):
        return lax.rem(s + 2 * n, n)

    def put(buf, s, rb, value):
        buf[ring(s, 3), rb, pl.ds(SIDE, LANES), :] = value
        buf[ring(s + 1, 3), rb, pl.ds(0, SIDE), :] = value[LANES - SIDE :]
        buf[ring(s - 1, 3), rb, pl.ds(SIDE + LANES, SIDE), :] = value[:SIDE]

    def add_squares(k, s, rb, plane):
        sq = (plane * plane).reshape(TILE // 8, 8, LANES)
        cut = HEAD // 8
        ok = (s >= 1) & (s <= strips)
        zero = jnp.zeros((8, LANES), jnp.float32)
        first = jnp.where(ok & (rb > 0), jnp.sum(sq[:cut], axis=0), zero)
        rest = jnp.where(ok & (rb < tiles - 1), jnp.sum(sq[cut:], axis=0), zero)
        acc[k] += first + rest

    def nat(buf, n, s, rb, shift=0):
        return buf[ring(s, n), pl.ds(pl.multiple_of(rb * TILE, TILE) + (TOP - HEAD) + shift, TILE), :]

    def nat_put(buf, n, s, rb, value):
        buf[ring(s, n), pl.ds(pl.multiple_of(rb * TILE, TILE) + (TOP - HEAD), TILE), :] = value

    def out_put(buf, s, rb, value):
        buf[ring(s, 3), pl.ds(pl.multiple_of(rb * TILE, TILE), TILE), :] = value

    def stage_a(s, rb):
        put(y1t, s, rb, five(lambda k: nat(xs, 5, s, rb, k), 1).T)

    def columns(buf, s, rb, step):
        return five(lambda k: buf[ring(s, 3), rb, pl.ds(SIDE + k, LANES), :], step)

    def stage_b(s, rb):
        value = columns(y1t, s, rb, 1) * (1.0 / 256)
        put(c1t, s, rb, value)
        value = value.T
        nat_put(c1, 3, s, rb, value)
        plane = nat(xs, 5, s, rb) - value
        out_put(o1, s, rb, plane)
        add_squares(0, s, rb, plane)

    def stage_c(s, rb):
        nat_put(z, 2, s, rb, columns(c1t, s, rb, 2).T)

    def stage_d(s, rb):
        value = five(lambda k: nat(z, 2, s, rb, k), 2) * (1.0 / 256)
        nat_put(c2, 3, s, rb, value)
        plane = nat(c1, 3, s, rb) - value
        out_put(o2, s, rb, plane)
        add_squares(1, s, rb, plane)

    def stage_e(s, rb):
        put(y3t, s, rb, five(lambda k: nat(c2, 3, s, rb, k), 4).T)

    def stage_f(s, rb):
        value = (columns(y3t, s, rb, 4) * (1.0 / 256)).T
        out_put(o4, s, rb, value)
        plane = nat(c2, 3, s, rb) - value
        out_put(o3, s, rb, plane)
        add_squares(2, s, rb, plane)

    stages = dict(a=stage_a, b=stage_b, c=stage_c, d=stage_d, e=stage_e, f=stage_f)

    def run(first, last, names, count=None):
        def outer(big, carry):
            boundary(big)

            def inner(r, c):
                for name in reversed(names):
                    stages[name](*place(name, big, r))
                return c

            return lax.fori_loop(0, tiles if count is None else count, inner, carry)

        lax.fori_loop(first, last, outer, 0)

    acc[...] = jnp.zeros_like(acc)
    fetch(jnp.int32(0), False)
    fetch(jnp.int32(1), False)
    run(0, 1, "a")
    run(1, 2, "ab")
    run(2, 4, "abcde")
    run(4, strips + 2, "abcdef")
    run(strips + 2, strips + 4, "bcdef")
    run(strips + 4, strips + 5, "cdef", SKEW["f"])
    boundary(jnp.int32(strips + 5))
    boundary(jnp.int32(strips + 6))
    squares[...] = acc[...]


def transform(x, top, bottom, sides):
    rows, cols = x.shape
    strips = cols // LANES
    assert rows % TILE == 0
    tiles = (rows + 2 * HEAD + TILE - 1) // TILE
    tall = tiles * TILE + 2 * (TOP - HEAD)
    hbm = pl.BlockSpec(memory_space=pl.ANY)
    vmem = pl.BlockSpec(memory_space=pltpu.VMEM)
    big = jax.ShapeDtypeStruct((rows, cols), jnp.float32)
    natural = lambda n: pltpu.VMEM((n, tall, LANES), jnp.float32)
    turned = pltpu.VMEM((3, tiles, LANES + 2 * SIDE, TILE), jnp.float32)
    out = pltpu.VMEM((3, tiles * TILE, LANES), jnp.float32)
    return pl.pallas_call(
        functools.partial(kernel, rows=rows, strips=strips),
        in_specs=[hbm, hbm, hbm, hbm],
        out_specs=[hbm, hbm, hbm, hbm, vmem],
        out_shape=[big, big, big, big, jax.ShapeDtypeStruct((3, 8, LANES), jnp.float32)],
        scratch_shapes=[
            natural(5), turned, turned, natural(3), natural(2), natural(3), turned, out, out, out, out,
            pltpu.VMEM((3, 8, LANES), jnp.float32),
            pltpu.SemaphoreType.DMA((5, 3)),
            pltpu.SemaphoreType.DMA((4, 3)),
        ],
        compiler_params=pltpu.CompilerParams(vmem_limit_bytes=56 * 1024 * 1024),
        name="starlet",
    )(x, top, bottom, sides)


def neighbours(first, last, axis):
    count = lax.axis_size(axis)
    up = [(i, i + 1) for i in range(count - 1)]
    down = [(i + 1, i) for i in range(count - 1)]
    return lax.ppermute(last, axis, up), lax.ppermute(first, axis, down)


def halo(x, axis, dim):
    length = x.shape[dim]
    take = lambda a, b: lax.slice_in_dim(x, a, b, axis=dim)
    before, after = neighbours(take(0, REACH), take(length - REACH, length), axis)
    pos, count = lax.axis_index(axis), lax.axis_size(axis)
    before = jnp.where(pos == 0, jnp.flip(take(1, REACH + 1), dim), before)
    after = jnp.where(pos == count - 1, jnp.flip(take(length - REACH - 1, length - 1), dim), after)
    return before, after


def total(value):
    for axis in ("cols", "rows"):
        size = lax.axis_size(axis)
        hop = 1
        while hop < size:
            value = value + lax.ppermute(value, axis, [(i, i ^ hop) for i in range(size)])
            hop *= 2
    return value


def on_device(cube):
    x = cube[0]
    rows, cols = x.shape
    above, below = halo(x, "rows", 0)
    edge = lambda a, b: jnp.concatenate([above[:, a:b], x[:, a:b], below[:, a:b]], axis=0)
    first, last = edge(0, REACH + 1), edge(cols - REACH - 1, cols)
    left, right = neighbours(first[:, :REACH], last[:, 1:], "cols")
    pos, count = lax.axis_index("cols"), lax.axis_size("cols")
    left = jnp.where(pos == 0, jnp.flip(first[:, 1:], 1), left)
    right = jnp.where(pos == count - 1, jnp.flip(last[:, :REACH], 1), right)
    extra = TOP - REACH
    top = jnp.pad(above, ((extra, 0), (0, 0)))
    bottom = jnp.pad(below, ((0, extra), (0, 0)))
    sides = jnp.stack([
        jnp.pad(left, ((extra, extra), (LANES - REACH, 0))),
        jnp.pad(right, ((extra, extra), (0, LANES - REACH))),
    ])
    w1, w2, w3, smooth, squares = transform(x, top, bottom, sides)
    pixels = float(lax.axis_size("rows") * lax.axis_size("cols") * rows * cols)
    sums = total(jnp.sum(squares, axis=(1, 2)))
    sigmas = jnp.sqrt(sums / pixels + 1e-06)[:, None]
    return w1[None], w2[None], w3[None], smooth[None], sigmas


def solution(mesh):
    whole = P(None, "rows", "cols")
    return jax.shard_map(
        on_device, mesh=mesh, in_specs=(whole,), out_specs=(whole, whole, whole, whole, P()), check_vma=False
    )
```

time: 549 us -> 127 us (0.23)
  other arithmetic: 308 us -> 2.87 us
  local copies, waits for them, and re-layouts: 149 us -> 11.5 us
  Pallas kernels: 0 us -> 78.9 us
  blocking collectives: 44.6 us -> 0 us
  starting transfers between devices: 35 us -> 20.9 us
    add x3 -> x4, other arithmetic: 152 us -> 0.01 us  [total(): value + lax.ppermute(value, axis, [(i, i ^ hop) for i in range(size)])]
    reduce_sum x3 -> x1, other arithmetic: 152 us -> 0.81 us  [on_device(): sums = total(jnp.sum(squares, axis=(1, 2)))]
    unnamed x5 -> x0, local copies, waits for them, and re-layouts: 93.2 us -> none
    pallas_call x0 -> x1, Pallas kernels: none -> 78.9 us  [transform(): pl.pallas_call(functools.partial(kernel, rows=rows, strips=strips), in_sp...]
    psum x1 -> x0, blocking collectives: 44.6 us -> none  [record(): square = lax.psum(square, ('rows', 'cols'))]
    rev x12 -> x4, local copies, waits for them, and re-layouts: 24.5 us -> 4.31 us  [the longest x1 1.58 us: on_device(): left = jnp.where(pos == 0, jnp.flip(first[:, 1:], 1), left)]
    slice x10 -> x14, local copies, waits for them, and re-layouts: 23.4 us -> 4.6 us  [the longest x3 2.19 us: on_device(): x[:, a:b]]
    ppermute x12 -> x9, starting transfers between devices: 35 us -> 20.9 us  [the longest x5 10.9 us: total(): lax.ppermute(value, axis, [(i, i ^ hop) for i in range(size)])]
  transfers between devices with their start and end apart: 12 -> 9, of which waited for: 3 -> 6; matrix products, arithmetic and copies ran while one was open for 17% -> 7% of each run, Pallas kernels for 0% -> 0%
where the time goes in v1:
time: 127 us; the launch traced here: 126 us
  Pallas kernels  78.9 us (62%)
  starting transfers between devices  20.9 us (16%)
  local copies, waits for them, and re-layouts  11.5 us (9%)
  waiting for transfers between devices  11.5 us (9%)
  other arithmetic  2.87 us (2%)
    pallas_call x1, Pallas kernels, transform(): pl.pallas_call(functools.partial(kernel, rows=rows, strips=strips), in_sp...  78.9 us
    ppermute x5, starting transfers between devices, total(): lax.ppermute(value, axis, [(i, i ^ hop) for i in range(size)])  10.9 us
    ppermute x4, starting transfers between devices, neighbours(): return (lax.ppermute(last, axis, up), lax.ppermute(first, axis, down))  10 us
    ppermute x5, waiting for transfers between devices, total(): lax.ppermute(value, axis, [(i, i ^ hop) for i in range(size)])  7.84 us
    ppermute x4, waiting for transfers between devices, neighbours(): return (lax.ppermute(last, axis, up), lax.ppermute(first, axis, down))  3.65 us
  transfers between devices with their start and end apart: 9, of which 6 were waited for; matrix products, arithmetic and copies ran while one was open for 7% of the time, Pallas kernels for 0%

profile of v1, /device:TPU:0, one launch (start us, length us, event | category | flops | bytes accessed | tf_op | source)
XLA Modules:
  0.0 126.4 jit_solution(10410184981481633997)
XLA Ops:
  0.6 1.3 %slice_bitcast_fusion = (f32[14,3072]{1,0:T(8,128)S(1)}, f32[14,3072]{1,0:T(8,128)S(1)}, f32[14,3072]{1,0:T(8,128)S(1)}, f32[14,3072]{1,0:T(8,128)S(1)}) fusion(f32[1,1536,3072]{2,1,0:T(8,128)} %param.1), kind=kLoop, calls=%fused_computation.5 | loop fusion | bytes 1376256 | tf_op jit(solution)/shard_map/slice | solution.py:209
  1.9 1.3 %collective-permute-start.1 = (f32[14,3072]{1,0:T(8,128)S(1)}, f32[14,3072]{1,0:T(8,128)S(1)}, u32[]{:S(2)}, u32[]{:S(2)}) collective-permute-start(f32[14,3072]{1,0:T(8,128)S(1)} %get-tuple-element.17), channel_id=1, source_target_pairs={{4,0},{8,4},{12,8},{16,12},{20,16},{24,20},{28,24},{5,1},{9,5},{13... | collective-permute-start | bytes 516104 | tf_op jit(solution)/shard_map/ppermute | solution.py:204
  3.2 5.5 %collective-permute-start = (f32[14,3072]{1,0:T(8,128)S(1)}, f32[14,3072]{1,0:T(8,128)S(1)}, u32[]{:S(2)}, u32[]{:S(2)}) collective-permute-start(f32[14,3072]{1,0:T(8,128)S(1)} %get-tuple-element.18), channel_id=1, source_target_pairs={{0,4},{4,8},{8,12},{12,16},{16,20},{20,24},{24,28},{1,5},{5,9},{9,... | collective-permute-start | bytes 516104 | tf_op jit(solution)/shard_map/ppermute | solution.py:204
  8.7 1.7 %fusion = (f32[1536,15]{1,0:T(8,128)S(1)}, f32[1536,15]{1,0:T(8,128)S(1)}) fusion(f32[1536,3072]{1,0:T(8,128)} %bitcast.19), kind=kLoop, calls=%fused_computation.12 | loop fusion | bytes 368640 | tf_op jit(solution)/shard_map/slice | solution.py:231
  10.4 0.6 rev.14
  11.0 0.6 rev.15
  11.6 0.3 copy.7
  11.8 0.3 copy.11
  12.1 0.0 collective-permute-done.1
  12.1 0.1 fusion.1
  12.2 0.1 copy.8
  12.3 0.1 copy.12
  12.4 3.6 %collective-permute-done = f32[14,3072]{1,0:T(8,128)S(1)} collective-permute-done((f32[14,3072]{1,0:T(8,128)S(1)}, f32[14,3072]{1,0:T(8,128)S(1)}, u32[]{:S(2)}, u32[]{:S(2)}) %collective-permute-start) | collective-permute-done | bytes 172064 | tf_op jit(solution)/shard_map/ppermute | solution.py:204
  16.1 0.1 fusion.2
  16.1 0.1 copy.6
  16.2 0.1 copy.10
  16.3 0.1 concatenate.7
  16.5 1.9 %collective-permute-start.2 = (f32[1564,14]{0,1:T(8,128)S(1)}, f32[1564,14]{0,1:T(8,128)S(1)}, u32[]{:S(2)}, u32[]{:S(2)}) collective-permute-start(f32[1564,14]{0,1:T(8,128)S(1)} %get-tuple-element.25), channel_id=1, source_target_pairs={{0,1},{1,2},{2,3},{4,5},{5,6},{6,7},{8,9},{9,10},{10,11},{12,13},{... | collective-permute-start | bytes 262760 | tf_op jit(solution)/shard_map/ppermute | solution.py:204
  18.4 0.1 concatenate.6
  18.5 0.7 pad.17.bottom
  19.3 0.7 pad.16.top
  20.0 1.3 %collective-permute-start.3 = (f32[1564,14]{0,1:T(8,128)S(1)}, f32[1564,14]{0,1:T(8,128)S(1)}, u32[]{:S(2)}, u32[]{:S(2)}) collective-permute-start(f32[1564,14]{0,1:T(8,128)S(1)} %get-tuple-element.28), channel_id=1, source_target_pairs={{1,0},{2,1},{3,2},{5,4},{6,5},{7,6},{9,8},{10,9},{11,10},{13,12},{... | collective-permute-start | bytes 262760 | tf_op jit(solution)/shard_map/ppermute | solution.py:204
  21.3 0.3 copy.9
  21.6 1.6 %rev.16 = f32[1564,14]{1,0:T(8,128)S(1)} reverse(f32[1564,14]{1,0:T(8,128)S(1)} %copy.9), dimensions={1} | reverse | bytes 175168 | tf_op jit(solution)/shard_map/jit(_flip)/rev | solution.py:235
  23.2 0.3 copy.14
  23.5 1.6 %rev.17 = f32[1564,14]{1,0:T(8,128)S(1)} reverse(f32[1564,14]{1,0:T(8,128)S(1)} %copy.14), dimensions={1} | reverse | bytes 175168 | tf_op jit(solution)/shard_map/jit(_flip)/rev | solution.py:236
  25.1 0.0 collective-permute-done.2
  25.1 0.3 copy.13
  25.4 0.1 broadcast_select_fusion.1
  25.5 0.0 collective-permute-done.3
  25.5 0.3 copy.15
  25.8 0.1 broadcast_select_fusion
  25.9 0.3 pad_bitcast_fusion
  26.2 1.3 %pad_maximum_fusion.sides = f32[2,1584,128]{2,1,0:T(8,128)} fusion(f32[1,1584,128]{2,1,0:T(8,128)S(1)} %get-tuple-element.29, f32[1,1584,128]{2,1,0:T(8,128)S(1)} %get-tuple-element.30), kind=kLoop, calls=%fused_computation | loop fusion | flops 405504 | bytes 3244032 | tf_op jit(solution)/shard_map/stack | solution.py:240
  27.5 78.9 %starlet.1 = (f32[1536,3072]{1,0:T(8,128)}, f32[1536,3072]{1,0:T(8,128)}, f32[1536,3072]{1,0:T(8,128)}, f32[1536,3072]{1,0:T(8,128)}, f32[3,8,128]{2,1,0:T(8,128)}) custom-call(f32[1536,3072]{1,0:T(8,128)} %bitcast.20, f32[24,3072]{1,0:T(8,128)} %pad.16.top, f32[24,3072]{1,0:T(8,128)} %pad.17.bottom, f32[2,1584,128]{2,1,0:T(8,128)} %pad_maximum_fusion.sides), custom_call_target="tpu_custom_call" | custom-call | tf_op jit(solution)/shard_map/starlet/pallas_call | solution.py:184
  106.3 0.8 reduce_sum.9
  107.1 2.2 %collective-permute-start.4 = (f32[3]{0:T(128)S(1)}, f32[3]{0:T(128)S(1)}, u32[]{:S(2)}, u32[]{:S(2)}) collective-permute-start(f32[3]{0:T(128)S(1)} %reduce_sum.9), channel_id=1, source_target_pairs={{0,1},{1,0},{2,3},{3,2},{4,5},{5,4},{6,7},{7,6},{8,9},{9,8},{10,11... | collective-permute-start | bytes 44 | tf_op jit(solution)/shard_map/ppermute | solution.py:222
  109.4 0.8 collective-permute-done.4
  110.2 2.0 %collective-permute-start.5 = (f32[3]{0:T(128)S(1)}, f32[3]{0:T(128)S(1)}, u32[]{:S(2)}, u32[]{:S(2)}) collective-permute-start(f32[3]{0:T(128)S(1)} %add.26), channel_id=1, source_target_pairs={{0,2},{1,3},{2,0},{3,1},{4,6},{5,7},{6,4},{7,5},{8,10},{9,11},{10,... | collective-permute-start | bytes 44 | tf_op jit(solution)/shard_map/ppermute | solution.py:222
  112.2 1.6 %collective-permute-done.5 = f32[3]{0:T(128)S(1)} collective-permute-done((f32[3]{0:T(128)S(1)}, f32[3]{0:T(128)S(1)}, u32[]{:S(2)}, u32[]{:S(2)}) %collective-permute-start.5) | collective-permute-done | bytes 44 | tf_op jit(solution)/shard_map/ppermute | solution.py:222
  113.8 2.5 %collective-permute-start.6 = (f32[3]{0:T(128)S(1)}, f32[3]{0:T(128)S(1)}, u32[]{:S(2)}, u32[]{:S(2)}) collective-permute-start(f32[3]{0:T(128)S(1)} %add.27), channel_id=1, source_target_pairs={{0,4},{4,0},{8,12},{12,8},{16,20},{20,16},{24,28},{28,24},{1,5},{5... | collective-permute-start | bytes 44 | tf_op jit(solution)/shard_map/ppermute | solution.py:222
  116.3 1.5 %collective-permute-done.6 = f32[3]{0:T(128)S(1)} collective-permute-done((f32[3]{0:T(128)S(1)}, f32[3]{0:T(128)S(1)}, u32[]{:S(2)}, u32[]{:S(2)}) %collective-permute-start.6) | collective-permute-done | bytes 44 | tf_op jit(solution)/shard_map/ppermute | solution.py:222
  117.8 1.6 %collective-permute-start.7 = (f32[3]{0:T(128)S(1)}, f32[3]{0:T(128)S(1)}, u32[]{:S(2)}, u32[]{:S(2)}) collective-permute-start(f32[3]{0:T(128)S(1)} %add.28), channel_id=1, source_target_pairs={{0,8},{4,12},{8,0},{12,4},{16,24},{20,28},{24,16},{28,20},{1,9},{5... | collective-permute-start | bytes 44 | tf_op jit(solution)/shard_map/ppermute | solution.py:222
  119.4 2.0 %collective-permute-done.7 = f32[3]{0:T(128)S(1)} collective-permute-done((f32[3]{0:T(128)S(1)}, f32[3]{0:T(128)S(1)}, u32[]{:S(2)}, u32[]{:S(2)}) %collective-permute-start.7) | collective-permute-done | bytes 44 | tf_op jit(solution)/shard_map/ppermute | solution.py:222
  121.4 2.6 %collective-permute-start.8 = (f32[3]{0:T(128)S(1)}, f32[3]{0:T(128)S(1)}, u32[]{:S(2)}, u32[]{:S(2)}) collective-permute-start(f32[3]{0:T(128)S(1)} %add.29), channel_id=1, source_target_pairs={{0,16},{4,20},{8,24},{12,28},{16,0},{20,4},{24,8},{28,12},{1,17},{... | collective-permute-start | bytes 44 | tf_op jit(solution)/shard_map/ppermute | solution.py:222
  124.0 1.9 %collective-permute-done.8 = f32[3]{0:T(128)S(1)} collective-permute-done((f32[3]{0:T(128)S(1)}, f32[3]{0:T(128)S(1)}, u32[]{:S(2)}, u32[]{:S(2)}) %collective-permute-start.8) | collective-permute-done | bytes 44 | tf_op jit(solution)/shard_map/ppermute | solution.py:222
  125.9 0.5 sqrt_bitcast_fusion
  (8 shorter events, 0.1 us)
Async XLA Ops:
  1.9 10.2 %collective-permute-start.1 = (f32[14,3072]{1,0:T(8,128)S(1)}, f32[14,3072]{1,0:T(8,128)S(1)}, u32[]{:S(2)}, u32[]{:S(2)}) collective-permute-start(f32[14,3072]{1,0:T(8,128)S(1)} %get-tuple-element.17), channel_id=1, source_target_pairs={{4,0},{8,4},{12,8},{16,12},{20,16},{24,20},{28,24},{5,1},{9,5},{13... | collective-permute-start | bytes 516104 | tf_op jit(solution)/shard_map/ppermute | solution.py:204
  3.2 12.8 %collective-permute-start = (f32[14,3072]{1,0:T(8,128)S(1)}, f32[14,3072]{1,0:T(8,128)S(1)}, u32[]{:S(2)}, u32[]{:S(2)}) collective-permute-start(f32[14,3072]{1,0:T(8,128)S(1)} %get-tuple-element.18), channel_id=1, source_target_pairs={{0,4},{4,8},{8,12},{12,16},{16,20},{20,24},{24,28},{1,5},{5,9},{9,... | collective-permute-start | bytes 516104 | tf_op jit(solution)/shard_map/ppermute | solution.py:204
  16.5 8.6 %collective-permute-start.2 = (f32[1564,14]{0,1:T(8,128)S(1)}, f32[1564,14]{0,1:T(8,128)S(1)}, u32[]{:S(2)}, u32[]{:S(2)}) collective-permute-start(f32[1564,14]{0,1:T(8,128)S(1)} %get-tuple-element.25), channel_id=1, source_target_pairs={{0,1},{1,2},{2,3},{4,5},{5,6},{6,7},{8,9},{9,10},{10,11},{12,13},{... | collective-permute-start | bytes 262760 | tf_op jit(solution)/shard_map/ppermute | solution.py:204
  20.0 5.5 %collective-permute-start.3 = (f32[1564,14]{0,1:T(8,128)S(1)}, f32[1564,14]{0,1:T(8,128)S(1)}, u32[]{:S(2)}, u32[]{:S(2)}) collective-permute-start(f32[1564,14]{0,1:T(8,128)S(1)} %get-tuple-element.28), channel_id=1, source_target_pairs={{1,0},{2,1},{3,2},{5,4},{6,5},{7,6},{9,8},{10,9},{11,10},{13,12},{... | collective-permute-start | bytes 262760 | tf_op jit(solution)/shard_map/ppermute | solution.py:204
  107.1 3.1 %collective-permute-start.4 = (f32[3]{0:T(128)S(1)}, f32[3]{0:T(128)S(1)}, u32[]{:S(2)}, u32[]{:S(2)}) collective-permute-start(f32[3]{0:T(128)S(1)} %reduce_sum.9), channel_id=1, source_target_pairs={{0,1},{1,0},{2,3},{3,2},{4,5},{5,4},{6,7},{7,6},{8,9},{9,8},{10,11... | collective-permute-start | bytes 44 | tf_op jit(solution)/shard_map/ppermute | solution.py:222
  110.2 3.6 %collective-permute-start.5 = (f32[3]{0:T(128)S(1)}, f32[3]{0:T(128)S(1)}, u32[]{:S(2)}, u32[]{:S(2)}) collective-permute-start(f32[3]{0:T(128)S(1)} %add.26), channel_id=1, source_target_pairs={{0,2},{1,3},{2,0},{3,1},{4,6},{5,7},{6,4},{7,5},{8,10},{9,11},{10,... | collective-permute-start | bytes 44 | tf_op jit(solution)/shard_map/ppermute | solution.py:222
  113.8 4.0 %collective-permute-start.6 = (f32[3]{0:T(128)S(1)}, f32[3]{0:T(128)S(1)}, u32[]{:S(2)}, u32[]{:S(2)}) collective-permute-start(f32[3]{0:T(128)S(1)} %add.27), channel_id=1, source_target_pairs={{0,4},{4,0},{8,12},{12,8},{16,20},{20,16},{24,28},{28,24},{1,5},{5... | collective-permute-start | bytes 44 | tf_op jit(solution)/shard_map/ppermute | solution.py:222
  117.8 3.6 %collective-permute-start.7 = (f32[3]{0:T(128)S(1)}, f32[3]{0:T(128)S(1)}, u32[]{:S(2)}, u32[]{:S(2)}) collective-permute-start(f32[3]{0:T(128)S(1)} %add.28), channel_id=1, source_target_pairs={{0,8},{4,12},{8,0},{12,4},{16,24},{20,28},{24,16},{28,20},{1,9},{5... | collective-permute-start | bytes 44 | tf_op jit(solution)/shard_map/ppermute | solution.py:222
  121.4 4.5 %collective-permute-start.8 = (f32[3]{0:T(128)S(1)}, f32[3]{0:T(128)S(1)}, u32[]{:S(2)}, u32[]{:S(2)}) collective-permute-start(f32[3]{0:T(128)S(1)} %add.29), channel_id=1, source_target_pairs={{0,16},{4,20},{8,24},{12,28},{16,0},{20,4},{24,8},{28,12},{1,17},{... | collective-permute-start | bytes 44 | tf_op jit(solution)/shard_map/ppermute | solution.py:222

commit v2 on v0

v2 whole, which is shorter than its diff:
```python
import functools

import jax
import jax.numpy as jnp
from jax import lax
from jax.experimental import pallas as pl
from jax.experimental.pallas import tpu as pltpu
from jax.sharding import PartitionSpec as P

LANES = 128
TILE = 128
REACH = 14
EDGE = 16
HEAD = 24
PAD = 8
SIDE = 8
RING = 4
LONG = 6


def five(load, step):
    a, b, c, d, e = (load(k * step) for k in (-2, -1, 0, 1, 2))
    return (a + e) + 4.0 * (b + d) + 6.0 * c


STAGES = "aAbBcCdeEfF"


def stage_lags(tiles):
    even = lambda n: n + n % 2
    lags = dict(a=0)
    after = dict(A=0, b=tiles, B=0, c=tiles, C=0, d=1, e=1, E=0, f=tiles, F=0)
    source = dict(A="a", b="A", B="b", c="b", C="c", d="C", e="d", E="e", f="E", F="f")
    for st in STAGES[1:]:
        lags[st] = even(lags[source[st]] + after[st] + 2)
    return lags


def kernel(x, top, bottom, left, right, first, last, w1, w2, w3, smooth, squares, xs, y1t, c1t, c1, z, c2, y3t, o1, o2, o3, o4,
           ya, zt, ye, c3t, acc, edge, isem, osem, *, rows, strips):
    tiles = (rows + HEAD + EDGE + TILE - 1) // TILE
    tall = tiles * TILE
    lags = stage_lags(tiles)
    ring, long = RING * tiles, LONG * tiles
    outs = ((o1, w1, "B"), (o2, w2, "d"), (o3, w3, "F"), (o4, smooth, "F"))

    def slot_of(s):
        return lax.rem(s, LONG)

    def in_copies(s):
        slot = slot_of(s)
        base = pl.multiple_of(slot * tall + PAD, 8)
        cols = pl.ds(pl.multiple_of((s - 1) * LANES, LANES), LANES)
        return (
            pltpu.make_async_copy(x.at[:, cols], xs.at[pl.ds(base + HEAD, rows), :], isem.at[slot, 0]),
            pltpu.make_async_copy(top.at[:, cols], xs.at[pl.ds(base + HEAD - EDGE, EDGE), :], isem.at[slot, 1]),
            pltpu.make_async_copy(bottom.at[:, cols], xs.at[pl.ds(base + HEAD + rows, EDGE), :], isem.at[slot, 2]),
        )

    row_pos, col_pos = lax.axis_index("rows"), lax.axis_index("cols")
    row_ends = (row_pos == 0, row_pos == lax.axis_size("rows") - 1)
    col_ends = (col_pos == 0, col_pos == lax.axis_size("cols") - 1)

    def build_side(side, s):
        got, own = ((left, first), (right, last))[side]

        edge[...] = got[...]

        @pl.when(col_ends[side])
        def _():
            for k in range(1, EDGE):
                to = EDGE - k if side == 0 else k - 1
                edge[pl.ds(to, 1), :] = own[pl.ds(k if side == 0 else EDGE - 1 - k, 1), :]

        base = pl.multiple_of(slot_of(s) * tall + PAD, 8)
        blank = jnp.zeros((LANES - EDGE, TILE), jnp.float32)

        def one(rb, c):
            at = pl.multiple_of(rb * TILE, TILE)
            part = edge[:, pl.ds(at, TILE)]
            part = jnp.concatenate([blank, part] if side == 0 else [part, blank], axis=0)
            xs[pl.ds(base + at, TILE), :] = part.T
            return c

        lax.fori_loop(0, tiles, one, 0)

    def mirror_rows(s):
        base = slot_of(s) * tall + PAD + HEAD

        @pl.when(row_ends[0])
        def _():
            for k in range(1, REACH + 1):
                xs[pl.ds(base - k, 1), :] = xs[pl.ds(base + k, 1), :]

        @pl.when(row_ends[1])
        def _():
            for k in range(1, REACH + 1):
                xs[pl.ds(base + rows - 1 + k, 1), :] = xs[pl.ds(base + rows - 1 - k, 1), :]

    def request(s):
        @pl.when((s >= 1) & (s <= strips))
        def _():
            for c in in_copies(s):
                c.start()

    def receive(s):
        for side, at in ((0, 0), (1, strips + 1)):

            @pl.when(s == at)
            def _():
                build_side(side, s)

        @pl.when((s >= 1) & (s <= strips))
        def _():
            for c in in_copies(s):
                c.wait()

        @pl.when(s <= strips + 1)
        def _():
            mirror_rows(s)

    def out_copy(k, s):
        buf, dst, _ = outs[k]
        slot = slot_of(s)
        base = pl.multiple_of(slot * tall + HEAD, 8)
        cols = pl.ds(pl.multiple_of((s - 1) * LANES, LANES), LANES)
        return pltpu.make_async_copy(buf.at[pl.ds(base, rows), :], dst.at[:, cols], osem.at[k, slot])

    def boundary(p):
        for u in (0, 1):
            request(2 * p + 2 + u)
        for u in (0, 1):
            receive(2 * p + u)
        for k, (_, _, st) in enumerate(outs):
            newest = 2 * p - 1 - -(-lags[st] // tiles)
            for s in (newest - 3, newest - 2):

                @pl.when((s >= 1) & (s <= strips))
                def _():
                    out_copy(k, s).wait()

            for s in (newest - 1, newest):

                @pl.when((s >= 1) & (s <= strips))
                def _():
                    out_copy(k, s).start()

    def wrap(i, n):
        return jnp.where(i < 0, i + n, i)

    class Place:
        def __init__(self, st, p, r, m, ml):
            lag = lags[st]
            self.short = wrap(m - lag % ring, ring)
            self.long = wrap(ml - lag % long, long)
            self.q = 2 * tiles * p + 2 * r - lag
            self.x = 2 * r + (-lag) % tiles

        def rows_at(self, u, buf_long=False):
            i = self.long if buf_long else self.short
            return pl.multiple_of(i * TILE, TILE) + u * TILE

        def turned_at(self, u, strip=0):
            if strip == 0:
                return pl.multiple_of(self.short * (LANES + 2 * SIDE), 8) + u * (LANES + 2 * SIDE)
            i = self.short + u + strip * tiles
            i = jnp.where(i >= ring, i - ring, i) if strip > 0 else wrap(i, ring)
            return pl.multiple_of(i * (LANES + 2 * SIDE), 8)

        def masks(self, u):
            q, rb = self.q + u, self.x + u
            for _ in range(3):
                rb = jnp.where(rb >= tiles, rb - tiles, rb)
            ok = (q >= tiles) & (q < tiles * (strips + 1))
            return ok & (rb > 0), ok & (rb < tiles - 1)

    def nat(buf, at, u, shift=0, is_long=False):
        return buf[pl.ds(at.rows_at(u, is_long) + PAD + shift, TILE), :]

    def nat_put(buf, at, u, value):
        buf[pl.ds(at.rows_at(u) + PAD, TILE), :] = value

    def out_put(buf, at, u, value):
        buf[pl.ds(at.rows_at(u, True), TILE), :] = value

    def put(buf, at, u, value):
        buf[pl.ds(at.turned_at(u) + SIDE, LANES), :] = value
        buf[pl.ds(at.turned_at(u, 1), SIDE), :] = value[LANES - SIDE :]
        buf[pl.ds(at.turned_at(u, -1) + SIDE + LANES, SIDE), :] = value[:SIDE]

    def columns(buf, at, u, step):
        return five(lambda k: buf[pl.ds(at.turned_at(u) + SIDE + k, LANES), :], step)

    def add_squares(k, at, u, plane):
        sq = (plane * plane).reshape(TILE // 8, 8, LANES)
        cut = HEAD // 8
        first_ok, rest_ok = at.masks(u)
        zero = jnp.zeros((8, LANES), jnp.float32)
        first = jnp.where(first_ok, jnp.sum(sq[:cut], axis=0), zero)
        rest = jnp.where(rest_ok, jnp.sum(sq[cut:], axis=0), zero)
        acc[k] += first + rest

    def hold(buf, u, value):
        buf[pl.ds(u * TILE, TILE), :] = value

    def held(buf, u):
        return buf[pl.ds(u * TILE, TILE), :].T

    def rows_a(at, u):
        hold(ya, u, five(lambda k: nat(xs, at, u, k, True), 1))

    def turn_a(at, u):
        put(y1t, at, u, held(ya, u))

    def cols_b(at, u):
        put(c1t, at, u, columns(y1t, at, u, 1) * (1.0 / 256))

    def turn_b(at, u):
        value = c1t[pl.ds(at.turned_at(u) + SIDE, LANES), :].T
        nat_put(c1, at, u, value)
        plane = nat(xs, at, u, 0, True) - value
        out_put(o1, at, u, plane)
        add_squares(0, at, u, plane)

    def cols_c(at, u):
        hold(zt, u, columns(c1t, at, u, 2))

    def turn_c(at, u):
        nat_put(z, at, u, held(zt, u))

    def rows_d(at, u):
        value = five(lambda k: nat(z, at, u, k), 2) * (1.0 / 256)
        nat_put(c2, at, u, value)
        plane = nat(c1, at, u) - value
        out_put(o2, at, u, plane)
        add_squares(1, at, u, plane)

    def rows_e(at, u):
        hold(ye, u, five(lambda k: nat(c2, at, u, k), 4))

    def turn_e(at, u):
        put(y3t, at, u, held(ye, u))

    def cols_f(at, u):
        hold(c3t, u, columns(y3t, at, u, 4) * (1.0 / 256))

    def turn_f(at, u):
        value = held(c3t, u)
        out_put(o4, at, u, value)
        plane = nat(c2, at, u) - value
        out_put(o3, at, u, plane)
        add_squares(2, at, u, plane)

    stages = dict(
        a=rows_a, A=turn_a, b=cols_b, B=turn_b, c=cols_c, C=turn_c, d=rows_d, e=rows_e, E=turn_e, f=cols_f, F=turn_f
    )

    def run(spans):
        def outer(p, carry):
            boundary(p)
            for lo, hi, names in spans:

                def inner(r, c, names=names):
                    m, ml = c
                    for name in reversed(names):
                        at = Place(name, p, r, m, ml)
                        for u in (0, 1):
                            stages[name](at, u)
                    m, ml = m + 2, ml + 2
                    return jnp.where(m >= ring, m - ring, m), jnp.where(ml >= long, ml - long, ml)

                carry = lax.fori_loop(lo, hi, inner, carry)
            return carry

        return outer

    acc[...] = jnp.zeros_like(acc)
    for u in (0, 1):
        request(jnp.int32(u))
    ends = {st: tiles * (strips + 2) + lag for st, lag in lags.items()}
    for st in "fF":
        ends[st] -= tiles
    starts = dict(lags, f=lags["f"] + tiles, F=lags["F"] + tiles)
    carry = (jnp.int32(0), jnp.int32(0))
    total = -(-ends["F"] // (2 * tiles))
    plan = []
    for p in range(total):
        spans = []
        for r in range(tiles):
            i = 2 * (tiles * p + r)
            names = "".join(st for st in STAGES if starts[st] - 1 <= i < ends[st])
            if spans and (spans[-1][2] == names or spans[-1][1] - spans[-1][0] < 2):
                names = "".join(st for st in STAGES if st in names or st in spans[-1][2])
                spans[-1] = (spans[-1][0], r + 1, names)
            elif names:
                spans.append((r, r + 1, names))
        if plan and plan[-1][2] == spans:
            plan[-1] = (plan[-1][0], p + 1, spans)
        else:
            plan.append((p, p + 1, spans))
    for lo, hi, spans in plan:
        carry = lax.fori_loop(lo, hi, run(spans), carry)
    for p in range(total, total + 4):
        boundary(jnp.int32(p))
    lane = lax.broadcasted_iota(jnp.int32, (1, LANES), 1)
    sums = jnp.zeros((1, LANES), jnp.float32)
    for k in range(3):
        sums = jnp.where(lane == k, jnp.sum(acc[k]), sums)
    squares[...] = jnp.broadcast_to(sums[None], squares.shape)


def transform(x, top, bottom, left, right, first, last, devices):
    rows, cols = x.shape
    strips = cols // LANES
    assert rows % TILE == 0 and cols % (2 * LANES) == 0
    tiles = (rows + HEAD + EDGE + TILE - 1) // TILE
    hbm = pl.BlockSpec(memory_space=pl.ANY)
    vmem = pl.BlockSpec(memory_space=pltpu.VMEM)
    big = jax.ShapeDtypeStruct((rows, cols), jnp.float32)
    natural = lambda n: pltpu.VMEM((n * tiles * TILE + 2 * PAD, LANES), jnp.float32)
    turned = pltpu.VMEM((RING * tiles * (LANES + 2 * SIDE), TILE), jnp.float32)
    held = pltpu.VMEM((2 * TILE, LANES), jnp.float32)
    out = pltpu.VMEM((LONG * tiles * TILE, LANES), jnp.float32)
    return pl.pallas_call(
        functools.partial(kernel, rows=rows, strips=strips),
        in_specs=[hbm, hbm, hbm, vmem, vmem, vmem, vmem],
        out_specs=[hbm, hbm, hbm, hbm, vmem],
        out_shape=[big, big, big, big, jax.ShapeDtypeStruct((devices, 1, LANES), jnp.float32)],
        scratch_shapes=[
            natural(LONG), turned, turned, natural(RING), natural(RING), natural(RING), turned, out, out, out, out,
            held, held, held, held,
            pltpu.VMEM((3, 8, LANES), jnp.float32),
            pltpu.VMEM((EDGE, tiles * TILE), jnp.float32),
            pltpu.SemaphoreType.DMA((LONG, 3)),
            pltpu.SemaphoreType.DMA((4, LONG)),
        ],
        compiler_params=pltpu.CompilerParams(vmem_limit_bytes=58 * 1024 * 1024),
        name="starlet",
    )(x, top, bottom, left, right, first, last)


def edge_kernel(left, right, first, last):
    for at in range(0, left.shape[0], TILE):
        first[:, at : at + TILE] = left[at : at + TILE, :].T[:EDGE]
        last[:, at : at + TILE] = right[at : at + TILE, :].T[LANES - EDGE :]


def turned_edges(x):
    rows, cols = x.shape
    strip = lambda i: pl.BlockSpec((rows, LANES), lambda g: (0, i))
    out = pl.BlockSpec((EDGE, rows), lambda g: (0, 0))
    shape = jax.ShapeDtypeStruct((EDGE, rows), jnp.float32)
    return pl.pallas_call(
        edge_kernel,
        grid=(1,),
        in_specs=[strip(0), strip(cols // LANES - 1)],
        out_specs=[out, out],
        out_shape=[shape, shape],
        cost_estimate=pl.CostEstimate(flops=0, bytes_accessed=8 * rows * LANES, transcendentals=0),
        name="edges",
    )(x, x)


def neighbours(first, last, axis):
    count = lax.axis_size(axis)
    up = [(i, i + 1) for i in range(count - 1)]
    down = [(i + 1, i) for i in range(count - 1)]
    return lax.ppermute(last, axis, up), lax.ppermute(first, axis, down)


def on_device(cube):
    x = cube[0]
    rows, cols = x.shape
    devices = lax.axis_size("rows") * lax.axis_size("cols")
    tall = (rows + HEAD + EDGE + TILE - 1) // TILE * TILE
    above, below = neighbours(x[:EDGE], x[rows - EDGE :], "rows")

    inner = turned_edges(x)

    def edge(mid, a, b):
        parts = [above[:, a:b].T, mid, below[:, a:b].T]
        return jnp.pad(jnp.concatenate(parts, axis=1), ((0, 0), (HEAD - EDGE, tall - rows - HEAD - EDGE)))

    first, last = edge(inner[0], 0, EDGE), edge(inner[1], cols - EDGE, cols)
    left, right = neighbours(first, last, "cols")
    w1, w2, w3, smooth, squares = transform(x, above, below, left, right, first, last, devices)
    sums = jnp.sum(lax.all_to_all(squares, ("rows", "cols"), 0, 0), axis=(0, 1))
    sigmas = jnp.sqrt(sums[:3] / float(devices * rows * cols) + 1e-06)[:, None]
    return w1[None], w2[None], w3[None], smooth[None], sigmas


def solution(mesh):
    whole = P(None, "rows", "cols")
    return jax.shard_map(
        on_device, mesh=mesh, in_specs=(whole,), out_specs=(whole, whole, whole, whole, P()), check_vma=False
    )
```

time: 549 us -> 103 us (0.19)
  other arithmetic: 308 us -> 0.57 us
  local copies, waits for them, and re-layouts: 149 us -> 4.33 us
  Pallas kernels: 0 us -> 64.5 us
  blocking collectives: 44.6 us -> 14.9 us
  starting transfers between devices: 35 us -> 10 us
    add x3 -> x0, other arithmetic: 152 us -> none  [filter_dim(): return outer + inner + part(2 * step, 2 * step) * 0.375]
    reduce_sum x3 -> x1, other arithmetic: 152 us -> 0.05 us  [on_device(): sums = jnp.sum(lax.all_to_all(squares, ('rows', 'cols'), 0, 0), axis=(0, 1))]
    unnamed x5 -> x16, local copies, waits for them, and re-layouts: 93.2 us -> 0.92 us
    pallas_call x0 -> x2, Pallas kernels: none -> 64.5 us  [the longest x1 61.9 us: transform(): pl.pallas_call(functools.partial(kernel, rows=rows, strips=strips), in_sp...]
    psum x1 -> x0, blocking collectives: 44.6 us -> none  [record(): square = lax.psum(square, ('rows', 'cols'))]
    ppermute x12 -> x4, starting transfers between devices: 35 us -> 10 us  [neighbours(): return (lax.ppermute(last, axis, up), lax.ppermute(first, axis, down))]
    rev x12 -> x0, local copies, waits for them, and re-layouts: 24.5 us -> none  [the longest x6 18.8 us: mirror_edges(): jnp.flip(lax.slice_in_dim(padded, length - 2 * width - 1, length - width...]
    slice x10 -> x3, local copies, waits for them, and re-layouts: 23.4 us -> 1.19 us  [the longest x1 1.05 us: on_device(): above, below = neighbours(x[:EDGE], x[rows - EDGE:], 'rows')]
  transfers between devices with their start and end apart: 12 -> 4, of which waited for: 3 -> 3; matrix products, arithmetic and copies ran while one was open for 17% -> 0% of each run, Pallas kernels for 0% -> 2%
where the time goes in v2:
time: 103 us
  Pallas kernels  64.5 us (63%)
  blocking collectives  14.9 us (14%)
  starting transfers between devices  10 us (10%)
  waiting for transfers between devices  7.6 us (7%)
  local copies, waits for them, and re-layouts  4.33 us (4%)
    pallas_call x1, Pallas kernels, transform(): pl.pallas_call(functools.partial(kernel, rows=rows, strips=strips), in_sp...  61.9 us
    all_to_all x1, blocking collectives, on_device(): sums = jnp.sum(lax.all_to_all(squares, ('rows', 'cols'), 0, 0), axis=(0, 1))  14.9 us
    ppermute x4, starting transfers between devices, neighbours(): return (lax.ppermute(last, axis, up), lax.ppermute(first, axis, down))  10 us
    ppermute x4, waiting for transfers between devices, neighbours(): return (lax.ppermute(last, axis, up), lax.ppermute(first, axis, down))  7.6 us
    pallas_call x1, Pallas kernels, turned_edges(): pl.pallas_call(edge_kernel, grid=(1,), in_specs=[strip(0), strip(cols //...  2.5 us
  transfers between devices with their start and end apart: 4, of which 3 were waited for; matrix products, arithmetic and copies ran while one was open for 0% of the time, Pallas kernels for 2%

profile of v2, /device:TPU:0, one launch (start us, length us, event | category | flops | bytes accessed | tf_op | source)
XLA Modules:
  0.0 102.6 jit_solution(6109111347264653663)
XLA Ops:
  0.6 1.1 %slice_bitcast_fusion = (f32[16,3072]{1,0:T(8,128)S(1)}, f32[16,3072]{1,0:T(8,128)S(1)}) fusion(f32[1,1536,3072]{2,1,0:T(8,128)} %param.1), kind=kLoop, calls=%fused_computation | loop fusion | bytes 786432 | tf_op jit(solution)/shard_map/slice | solution.py:376
  1.7 1.3 %collective-permute-start.1 = (f32[16,3072]{1,0:T(8,128)S(1)}, f32[16,3072]{1,0:T(8,128)S(1)}, u32[]{:S(2)}, u32[]{:S(2)}) collective-permute-start(f32[16,3072]{1,0:T(8,128)S(1)} %get-tuple-element.19), channel_id=1, source_target_pairs={{4,0},{8,4},{12,8},{16,12},{20,16},{24,20},{28,24},{5,1},{9,5},{13... | collective-permute-start | bytes 589832 | tf_op jit(solution)/shard_map/ppermute | solution.py:368
  3.0 5.5 %collective-permute-start = (f32[16,3072]{1,0:T(8,128)S(1)}, f32[16,3072]{1,0:T(8,128)S(1)}, u32[]{:S(2)}, u32[]{:S(2)}) collective-permute-start(f32[16,3072]{1,0:T(8,128)S(1)} %get-tuple-element.20), channel_id=1, source_target_pairs={{0,4},{4,8},{8,12},{12,16},{16,20},{20,24},{24,28},{1,5},{5,9},{9,... | collective-permute-start | bytes 589832 | tf_op jit(solution)/shard_map/ppermute | solution.py:368
  8.5 2.5 %edges.1 = (f32[16,1536]{1,0:T(8,128)}, f32[16,1536]{1,0:T(8,128)}) custom-call(f32[1536,3072]{1,0:T(8,128)} %bitcast.15, f32[1536,3072]{1,0:T(8,128)} %bitcast.16), custom_call_target="tpu_custom_call" | custom-call | bytes 1572864 | tf_op jit(solution)/shard_map/edges/pallas_call | solution.py:353
  11.0 0.4 collective-permute-done.1.bottom
  11.5 0.0 copy-start.2
  11.5 0.1 fusion
  11.5 0.1 copy.17
  11.6 0.1 copy.15
  11.7 4.1 %collective-permute-done.top = f32[16,3072]{1,0:T(8,128)S(1)} collective-permute-done((f32[16,3072]{1,0:T(8,128)S(1)}, f32[16,3072]{1,0:T(8,128)S(1)}, u32[]{:S(2)}, u32[]{:S(2)}) %collective-permute-start) | collective-permute-done | bytes 196640 | tf_op jit(solution)/shard_map/ppermute | solution.py:368
  15.8 0.0 copy-start.3
  15.8 0.1 fusion.1
  15.9 0.1 copy.16
  16.0 0.1 copy.14
  16.0 1.0 concatenate.7
  17.0 0.1 pad.8.first
  17.1 0.0 copy-start
  17.1 1.0 %concatenate.6 = f32[16,1568]{1,0:T(8,128)S(1)} concatenate(f32[16,16]{1,0:T(8,128)S(1)} %bitcast.20, f32[16,1536]{1,0:T(8,128)} %get-tuple-element.12, f32[16,16]{1,0:T(8,128)S(1)} %bitcast.18), dimensions={1} | concatenate | bytes 200704 | tf_op jit(solution)/shard_map/concatenate | solution.py:382
  18.2 0.1 pad.7.last
  18.3 0.0 copy-start.1
  18.3 1.9 %collective-permute-start.2 = (f32[16,1664]{1,0:T(8,128)S(1)}, f32[16,1664]{1,0:T(8,128)S(1)}, u32[]{:S(2)}, u32[]{:S(2)}) collective-permute-start(f32[16,1664]{1,0:T(8,128)S(1)} %pad.7.last), channel_id=1, source_target_pairs={{0,1},{1,2},{2,3},{4,5},{5,6},{6,7},{8,9},{9,10},{10,11},{12,13},{... | collective-permute-start | bytes 319496 | tf_op jit(solution)/shard_map/ppermute | solution.py:368
  20.2 1.3 %collective-permute-start.3 = (f32[16,1664]{1,0:T(8,128)S(1)}, f32[16,1664]{1,0:T(8,128)S(1)}, u32[]{:S(2)}, u32[]{:S(2)}) collective-permute-start(f32[16,1664]{1,0:T(8,128)S(1)} %pad.8.first), channel_id=1, source_target_pairs={{1,0},{2,1},{3,2},{5,4},{6,5},{7,6},{9,8},{10,9},{11,10},{13,12},{... | collective-permute-start | bytes 319496 | tf_op jit(solution)/shard_map/ppermute | solution.py:368
  21.5 0.0 collective-permute-done.2.left
  21.5 0.0 copy-start.4
  21.5 3.0 %collective-permute-done.3.right = f32[16,1664]{1,0:T(8,128)S(1)} collective-permute-done((f32[16,1664]{1,0:T(8,128)S(1)}, f32[16,1664]{1,0:T(8,128)S(1)}, u32[]{:S(2)}, u32[]{:S(2)}) %collective-permute-start.3) | collective-permute-done | bytes 106528 | tf_op jit(solution)/shard_map/ppermute | solution.py:368
  24.6 0.0 copy-done.2
  24.6 0.0 copy-done.3
  24.6 0.0 copy-done
  24.6 0.0 copy-done.1
  24.6 0.0 copy-done.4
  24.6 0.0 copy-start.5
  24.6 0.6 copy-done.5
  25.2 61.9 %starlet.1 = (f32[1536,3072]{1,0:T(8,128)}, f32[1536,3072]{1,0:T(8,128)}, f32[1536,3072]{1,0:T(8,128)}, f32[1536,3072]{1,0:T(8,128)}, f32[32,1,128]{2,1,0:T(1,128)}) custom-call(f32[1536,3072]{1,0:T(8,128)} %bitcast.17, f32[16,3072]{1,0:T(8,128)} %copy-done.3, f32[16,3072]{1,0:T(8,128)} %copy-done.2, f32[16,1664]{1,0:T(8,128)} %copy-done.4, ...), custom_call_target="tpu_custom_call" | custom-call | tf_op jit(solution)/shard_map/starlet/pallas_call | solution.py:324
  87.2 14.9 %all_to_all.5 = f32[32,1,128]{2,1,0:T(1,128)S(1)} all-to-all(f32[32,1,128]{2,1,0:T(1,128)} %get-tuple-element.18), channel_id=1, replica_groups=mesh['rows'=8,'cols'=4] {'rows','cols'}, dimensions={0} | all-to-all | bytes 32768 | tf_op jit(solution)/shard_map/all_to_all | solution.py:387
  102.0 0.1 reduce_sum.9
  102.1 0.5 sqrt_bitcast_fusion
Async XLA Ops:
  1.7 9.8 %collective-permute-start.1 = (f32[16,3072]{1,0:T(8,128)S(1)}, f32[16,3072]{1,0:T(8,128)S(1)}, u32[]{:S(2)}, u32[]{:S(2)}) collective-permute-start(f32[16,3072]{1,0:T(8,128)S(1)} %get-tuple-element.19), channel_id=1, source_target_pairs={{4,0},{8,4},{12,8},{16,12},{20,16},{24,20},{28,24},{5,1},{9,5},{13... | collective-permute-start | bytes 589832 | tf_op jit(solution)/shard_map/ppermute | solution.py:368
  3.0 12.8 %collective-permute-start = (f32[16,3072]{1,0:T(8,128)S(1)}, f32[16,3072]{1,0:T(8,128)S(1)}, u32[]{:S(2)}, u32[]{:S(2)}) collective-permute-start(f32[16,3072]{1,0:T(8,128)S(1)} %get-tuple-element.20), channel_id=1, source_target_pairs={{0,4},{4,8},{8,12},{12,16},{16,20},{20,24},{24,28},{1,5},{5,9},{9,... | collective-permute-start | bytes 589832 | tf_op jit(solution)/shard_map/ppermute | solution.py:368
  11.5 13.1 %copy-start.2 = (f32[16,3072]{1,0:T(8,128)}, f32[16,3072]{1,0:T(8,128)S(1)}, u32[]{:S(2)}) copy-start(f32[16,3072]{1,0:T(8,128)S(1)} %collective-permute-done.1.bottom) | copy-start | bytes 589828
  15.8 8.7 %copy-start.3 = (f32[16,3072]{1,0:T(8,128)}, f32[16,3072]{1,0:T(8,128)S(1)}, u32[]{:S(2)}) copy-start(f32[16,3072]{1,0:T(8,128)S(1)} %collective-permute-done.top) | copy-start | bytes 589828
  17.1 7.4 %copy-start = (f32[16,1664]{1,0:T(8,128)}, f32[16,1664]{1,0:T(8,128)S(1)}, u32[]{:S(2)}) copy-start(f32[16,1664]{1,0:T(8,128)S(1)} %pad.8.first) | copy-start | bytes 319492
  18.3 6.3 %copy-start.1 = (f32[16,1664]{1,0:T(8,128)}, f32[16,1664]{1,0:T(8,128)S(1)}, u32[]{:S(2)}) copy-start(f32[16,1664]{1,0:T(8,128)S(1)} %pad.7.last) | copy-start | bytes 319492
  18.3 3.2 %collective-permute-start.2 = (f32[16,1664]{1,0:T(8,128)S(1)}, f32[16,1664]{1,0:T(8,128)S(1)}, u32[]{:S(2)}, u32[]{:S(2)}) collective-permute-start(f32[16,1664]{1,0:T(8,128)S(1)} %pad.7.last), channel_id=1, source_target_pairs={{0,1},{1,2},{2,3},{4,5},{5,6},{6,7},{8,9},{9,10},{10,11},{12,13},{... | collective-permute-start | bytes 319496 | tf_op jit(solution)/shard_map/ppermute | solution.py:368
  20.2 4.3 %collective-permute-start.3 = (f32[16,1664]{1,0:T(8,128)S(1)}, f32[16,1664]{1,0:T(8,128)S(1)}, u32[]{:S(2)}, u32[]{:S(2)}) collective-permute-start(f32[16,1664]{1,0:T(8,128)S(1)} %pad.8.first), channel_id=1, source_target_pairs={{1,0},{2,1},{3,2},{5,4},{6,5},{7,6},{9,8},{10,9},{11,10},{13,12},{... | collective-permute-start | bytes 319496 | tf_op jit(solution)/shard_map/ppermute | solution.py:368
  21.5 3.0 %copy-start.4 = (f32[16,1664]{1,0:T(8,128)}, f32[16,1664]{1,0:T(8,128)S(1)}, u32[]{:S(2)}) copy-start(f32[16,1664]{1,0:T(8,128)S(1)} %collective-permute-done.2.left) | copy-start | bytes 319492
  24.6 0.6 copy-start.5

commit v3 on v2

--- a/solution.py
+++ b/solution.py
@@ -63,26 +63,25 @@
 
     def build_side(side, s):
         got, own = ((left, first), (right, last))[side]
-
         edge[...] = got[...]
 
         @pl.when(col_ends[side])
         def _():
             for k in range(1, EDGE):
-                to = EDGE - k if side == 0 else k - 1
-                edge[pl.ds(to, 1), :] = own[pl.ds(k if side == 0 else EDGE - 1 - k, 1), :]
-
-        base = pl.multiple_of(slot_of(s) * tall + PAD, 8)
+                at = EDGE - k if side == 0 else k - 1
+                edge[pl.ds(at, 1), :] = own[pl.ds(k if side == 0 else EDGE - 1 - k, 1), :]
+
+        base = pl.multiple_of(slot_of(s) * tall + PAD + HEAD, 8)
         blank = jnp.zeros((LANES - EDGE, TILE), jnp.float32)
 
-        def one(rb, c):
-            at = pl.multiple_of(rb * TILE, TILE)
-            part = edge[:, pl.ds(at, TILE)]
-            part = jnp.concatenate([blank, part] if side == 0 else [part, blank], axis=0)
-            xs[pl.ds(base + at, TILE), :] = part.T
-            return c
-
-        lax.fori_loop(0, tiles, one, 0)
+        def turn(part):
+            return jnp.concatenate([blank, part] if side == 0 else [part, blank], axis=0).T
+
+        for at in range(0, rows, TILE):
+            xs[pl.ds(base + at, TILE), :] = turn(edge[:, at : at + TILE])
+        ends = turn(edge[:, rows:])
+        xs[pl.ds(base - EDGE, EDGE), :] = ends[:EDGE]
+        xs[pl.ds(base + rows, EDGE), :] = ends[EDGE : 2 * EDGE]
 
     def mirror_rows(s):
         base = slot_of(s) * tall + PAD + HEAD
@@ -97,27 +96,22 @@
             for k in range(1, REACH + 1):
                 xs[pl.ds(base + rows - 1 + k, 1), :] = xs[pl.ds(base + rows - 1 - k, 1), :]
 
+    def guarded(fn, p, span, ahead):
+        lo, hi = 2 * span[0] + ahead, 2 * (span[1] - 1) + ahead
+        s = 2 * p + ahead
+        if lo >= 1 and hi <= strips:
+            fn(s)
+        elif hi >= 1 and lo <= strips:
+            pl.when((s >= 1) & (s <= strips))(lambda: fn(s))
+
     def request(s):
-        @pl.when((s >= 1) & (s <= strips))
-        def _():
-            for c in in_copies(s):
-                c.start()
+        for c in in_copies(s):
+            c.start()
 
     def receive(s):
-        for side, at in ((0, 0), (1, strips + 1)):
-
-            @pl.when(s == at)
-            def _():
-                build_side(side, s)
-
-        @pl.when((s >= 1) & (s <= strips))
-        def _():
-            for c in in_copies(s):
-                c.wait()
-
-        @pl.when(s <= strips + 1)
-        def _():
-            mirror_rows(s)
+        for c in in_copies(s):
+            c.wait()
+        mirror_rows(s)
 
     def out_copy(k, s):
         buf, dst, _ = outs[k]
@@ -126,24 +120,24 @@
         cols = pl.ds(pl.multiple_of((s - 1) * LANES, LANES), LANES)
         return pltpu.make_async_copy(buf.at[pl.ds(base, rows), :], dst.at[:, cols], osem.at[k, slot])
 
-    def boundary(p):
+    def boundary(p, span):
+        for u in (2, 3):
+            guarded(request, p, span, u)
         for u in (0, 1):
-            request(2 * p + 2 + u)
-        for u in (0, 1):
-            receive(2 * p + u)
+            guarded(receive, p, span, u)
+        if span[0] <= strips // 2 < span[1]:
+
+            @pl.when(p == strips // 2)
+            def _():
+                build_side(1, strips + 1)
+                mirror_rows(strips + 1)
+
         for k, (_, _, st) in enumerate(outs):
-            newest = 2 * p - 1 - -(-lags[st] // tiles)
-            for s in (newest - 3, newest - 2):
-
-                @pl.when((s >= 1) & (s <= strips))
-                def _():
-                    out_copy(k, s).wait()
-
-            for s in (newest - 1, newest):
-
-                @pl.when((s >= 1) & (s <= strips))
-                def _():
-                    out_copy(k, s).start()
+            newest = -1 - -(-lags[st] // tiles)
+            for ahead in (newest - 3, newest - 2):
+                guarded(lambda s: out_copy(k, s).wait(), p, span, ahead)
+            for ahead in (newest - 1, newest):
+                guarded(lambda s: out_copy(k, s).start(), p, span, ahead)
 
     def wrap(i, n):
         return jnp.where(i < 0, i + n, i)
@@ -255,9 +249,9 @@
         a=rows_a, A=turn_a, b=cols_b, B=turn_b, c=cols_c, C=turn_c, d=rows_d, e=rows_e, E=turn_e, f=cols_f, F=turn_f
     )
 
-    def run(spans):
+    def run(spans, within):
         def outer(p, carry):
-            boundary(p)
+            boundary(p, within)
             for lo, hi, names in spans:
 
                 def inner(r, c, names=names):
@@ -275,8 +269,9 @@
         return outer
 
     acc[...] = jnp.zeros_like(acc)
-    for u in (0, 1):
-        request(jnp.int32(u))
+    request(jnp.int32(1))
+    build_side(0, jnp.int32(0))
+    mirror_rows(jnp.int32(0))
     ends = {st: tiles * (strips + 2) + lag for st, lag in lags.items()}
     for st in "fF":
         ends[st] -= tiles
@@ -294,14 +289,16 @@
                 spans[-1] = (spans[-1][0], r + 1, names)
             elif names:
                 spans.append((r, r + 1, names))
-        if plan and plan[-1][2] == spans:
-            plan[-1] = (plan[-1][0], p + 1, spans)
+        oldest = 2 * p - 4 - max(-(-lags[st] // tiles) for _, _, st in outs)
+        key = (spans, oldest >= 1, 2 * p + 3 <= strips)
+        if plan and plan[-1][2] == key:
+            plan[-1] = (plan[-1][0], p + 1, key)
         else:
-            plan.append((p, p + 1, spans))
-    for lo, hi, spans in plan:
-        carry = lax.fori_loop(lo, hi, run(spans), carry)
+            plan.append((p, p + 1, key))
+    for lo, hi, key in plan:
+        carry = lax.fori_loop(lo, hi, run(key[0], (lo, hi)), carry)
     for p in range(total, total + 4):
-        boundary(jnp.int32(p))
+        boundary(jnp.int32(p), (p, p + 1))
     lane = lax.broadcasted_iota(jnp.int32, (1, LANES), 1)
     sums = jnp.zeros((1, LANES), jnp.float32)
     for k in range(3):
@@ -309,7 +306,7 @@
     squares[...] = jnp.broadcast_to(sums[None], squares.shape)
 
 
-def transform(x, top, bottom, left, right, first, last, devices):
+def transform(x, rims, sides, devices):
     rows, cols = x.shape
     strips = cols // LANES
     assert rows % TILE == 0 and cols % (2 * LANES) == 0
@@ -323,33 +320,35 @@
     out = pltpu.VMEM((LONG * tiles * TILE, LANES), jnp.float32)
     return pl.pallas_call(
         functools.partial(kernel, rows=rows, strips=strips),
-        in_specs=[hbm, hbm, hbm, vmem, vmem, vmem, vmem],
+        in_specs=[hbm, hbm, hbm] + [vmem] * 4,
         out_specs=[hbm, hbm, hbm, hbm, vmem],
         out_shape=[big, big, big, big, jax.ShapeDtypeStruct((devices, 1, LANES), jnp.float32)],
         scratch_shapes=[
             natural(LONG), turned, turned, natural(RING), natural(RING), natural(RING), turned, out, out, out, out,
             held, held, held, held,
             pltpu.VMEM((3, 8, LANES), jnp.float32),
-            pltpu.VMEM((EDGE, tiles * TILE), jnp.float32),
+            pltpu.VMEM((EDGE, rows + LANES), jnp.float32),
             pltpu.SemaphoreType.DMA((LONG, 3)),
             pltpu.SemaphoreType.DMA((4, LONG)),
         ],
         compiler_params=pltpu.CompilerParams(vmem_limit_bytes=58 * 1024 * 1024),
         name="starlet",
-    )(x, top, bottom, left, right, first, last)
+    )(x, *rims, *sides)
 
 
 def edge_kernel(left, right, first, last):
     for at in range(0, left.shape[0], TILE):
         first[:, at : at + TILE] = left[at : at + TILE, :].T[:EDGE]
         last[:, at : at + TILE] = right[at : at + TILE, :].T[LANES - EDGE :]
+    for ref in (first, last):
+        ref[:, left.shape[0] :] = jnp.zeros((EDGE, LANES), jnp.float32)
 
 
 def turned_edges(x):
     rows, cols = x.shape
     strip = lambda i: pl.BlockSpec((rows, LANES), lambda g: (0, i))
-    out = pl.BlockSpec((EDGE, rows), lambda g: (0, 0))
-    shape = jax.ShapeDtypeStruct((EDGE, rows), jnp.float32)
+    out = pl.BlockSpec((EDGE, rows + LANES), lambda g: (0, 0))
+    shape = jax.ShapeDtypeStruct((EDGE, rows + LANES), jnp.float32)
     return pl.pallas_call(
         edge_kernel,
         grid=(1,),
@@ -372,18 +371,17 @@
     x = cube[0]
     rows, cols = x.shape
     devices = lax.axis_size("rows") * lax.axis_size("cols")
-    tall = (rows + HEAD + EDGE + TILE - 1) // TILE * TILE
+    first, last = turned_edges(x)
     above, below = neighbours(x[:EDGE], x[rows - EDGE :], "rows")
 
-    inner = turned_edges(x)
-
-    def edge(mid, a, b):
-        parts = [above[:, a:b].T, mid, below[:, a:b].T]
-        return jnp.pad(jnp.concatenate(parts, axis=1), ((0, 0), (HEAD - EDGE, tall - rows - HEAD - EDGE)))
-
-    first, last = edge(inner[0], 0, EDGE), edge(inner[1], cols - EDGE, cols)
+    def cornered(edge, a, b):
+        both = jnp.concatenate([above[:, a:b].T, below[:, a:b].T], axis=1)
+        both = jnp.pad(both, ((0, 0), (0, LANES - 2 * EDGE)))
+        return lax.dynamic_update_slice(edge, both, (0, rows))
+
+    first, last = cornered(first, 0, EDGE), cornered(last, cols - EDGE, cols)
     left, right = neighbours(first, last, "cols")
-    w1, w2, w3, smooth, squares = transform(x, above, below, left, right, first, last, devices)
+    w1, w2, w3, smooth, squares = transform(x, (above, below), (left, right, first, last), devices)
     sums = jnp.sum(lax.all_to_all(squares, ("rows", "cols"), 0, 0), axis=(0, 1))
     sigmas = jnp.sqrt(sums[:3] / float(devices * rows * cols) + 1e-06)[:, None]
     return w1[None], w2[None], w3[None], smooth[None], sigmas

time: 103 us -> 100 us (0.971)
  local copies, waits for them, and re-layouts: 4.33 us -> 2.12 us
  Pallas kernels: 64.5 us -> 62.7 us
  other arithmetic: 0.57 us -> 1.92 us
    concatenate x2 -> x0, local copies, waits for them, and re-layouts: 2.04 us -> none  [edge(): jnp.concatenate(parts, axis=1)]
    pallas_call x1, Pallas kernels: 61.9 us -> 60.2 us  [transform(): pl.pallas_call(functools.partial(kernel, rows=rows, strips=strips), in_sp...]
    dynamic_update_slice x0 -> x2, other arithmetic: none -> 1.35 us  [cornered(): return lax.dynamic_update_slice(edge, both, (0, rows))]
  transfers between devices with their start and end apart: 4 -> 4, of which waited for: 3 -> 3; matrix products, arithmetic and copies ran while one was open for 0% -> 1% of each run, Pallas kernels for 2% -> 3%
where the time goes in v3:
time: 100 us
  Pallas kernels  62.7 us (63%)
  blocking collectives  14.9 us (15%)
  starting transfers between devices  10 us (10%)
  waiting for transfers between devices  7.8 us (8%)
  local copies, waits for them, and re-layouts  2.12 us (2%)
  other arithmetic  1.92 us (2%)
    pallas_call x1, Pallas kernels, transform(): pl.pallas_call(functools.partial(kernel, rows=rows, strips=strips), in_sp...  60.2 us
    all_to_all x1, blocking collectives, on_device(): sums = jnp.sum(lax.all_to_all(squares, ('rows', 'cols'), 0, 0), axis=(0, 1))  14.9 us
    ppermute x4, starting transfers between devices, neighbours(): return (lax.ppermute(last, axis, up), lax.ppermute(first, axis, down))  10 us
    ppermute x4, waiting for transfers between devices, neighbours(): return (lax.ppermute(last, axis, up), lax.ppermute(first, axis, down))  7.8 us
    pallas_call x1, Pallas kernels, turned_edges(): pl.pallas_call(edge_kernel, grid=(1,), in_specs=[strip(0), strip(cols //...  2.52 us
  transfers between devices with their start and end apart: 4, of which 3 were waited for; matrix products, arithmetic and copies ran while one was open for 1% of the time, Pallas kernels for 3%

profile of v3, /device:TPU:0, one launch (start us, length us, event | category | flops | bytes accessed | tf_op | source)
XLA Modules:
  0.0 100.2 jit_solution(16531530026340705817)
XLA Ops:
  0.6 1.1 %slice_bitcast_fusion = (f32[16,3072]{1,0:T(8,128)S(1)}, f32[16,3072]{1,0:T(8,128)S(1)}) fusion(f32[1,1536,3072]{2,1,0:T(8,128)} %param.1), kind=kLoop, calls=%fused_computation | loop fusion | bytes 786432 | tf_op jit(solution)/shard_map/slice | solution.py:375
  1.7 1.3 %collective-permute-start.1 = (f32[16,3072]{1,0:T(8,128)S(1)}, f32[16,3072]{1,0:T(8,128)S(1)}, u32[]{:S(2)}, u32[]{:S(2)}) collective-permute-start(f32[16,3072]{1,0:T(8,128)S(1)} %get-tuple-element.19), channel_id=1, source_target_pairs={{4,0},{8,4},{12,8},{16,12},{20,16},{24,20},{28,24},{5,1},{9,5},{13... | collective-permute-start | bytes 589832 | tf_op jit(solution)/shard_map/ppermute | solution.py:367
  3.0 5.5 %collective-permute-start = (f32[16,3072]{1,0:T(8,128)S(1)}, f32[16,3072]{1,0:T(8,128)S(1)}, u32[]{:S(2)}, u32[]{:S(2)}) collective-permute-start(f32[16,3072]{1,0:T(8,128)S(1)} %get-tuple-element.20), channel_id=1, source_target_pairs={{0,4},{4,8},{8,12},{12,16},{16,20},{20,24},{24,28},{1,5},{5,9},{9,... | collective-permute-start | bytes 589832 | tf_op jit(solution)/shard_map/ppermute | solution.py:367
  8.5 2.5 %edges.1 = (f32[16,1664]{1,0:T(8,128)}, f32[16,1664]{1,0:T(8,128)}) custom-call(f32[1536,3072]{1,0:T(8,128)} %bitcast.15, f32[1536,3072]{1,0:T(8,128)} %bitcast.16), custom_call_target="tpu_custom_call" | custom-call | bytes 1572864 | tf_op jit(solution)/shard_map/edges/pallas_call | solution.py:352
  11.0 0.4 collective-permute-done.1.bottom
  11.5 0.0 copy-start
  11.5 0.1 fusion.3
  11.5 0.1 copy.17
  11.6 0.1 copy.15
  11.7 4.1 %collective-permute-done.top = f32[16,3072]{1,0:T(8,128)S(1)} collective-permute-done((f32[16,3072]{1,0:T(8,128)S(1)}, f32[16,3072]{1,0:T(8,128)S(1)}, u32[]{:S(2)}, u32[]{:S(2)}) %collective-permute-start) | collective-permute-done | bytes 196640 | tf_op jit(solution)/shard_map/ppermute | solution.py:367
  15.8 0.0 copy-start.1
  15.8 0.1 fusion.2
  15.9 0.1 copy.16
  16.0 0.1 copy.14
  16.0 0.7 fusion.1.last
  16.7 1.9 %collective-permute-start.2 = (f32[16,1664]{1,0:T(8,128)}, f32[16,1664]{1,0:T(8,128)S(1)}, u32[]{:S(2)}, u32[]{:S(2)}) collective-permute-start(f32[16,1664]{1,0:T(8,128)} %fusion.1.last), channel_id=1, source_target_pairs={{0,1},{1,2},{2,3},{4,5},{5,6},{6,7},{8,9},{9,10},{10,11},{12,13},{... | collective-permute-start | bytes 319496 | tf_op jit(solution)/shard_map/ppermute | solution.py:367
  18.6 0.7 fusion.first
  19.3 1.3 %collective-permute-start.3 = (f32[16,1664]{1,0:T(8,128)}, f32[16,1664]{1,0:T(8,128)S(1)}, u32[]{:S(2)}, u32[]{:S(2)}) collective-permute-start(f32[16,1664]{1,0:T(8,128)} %fusion.first), channel_id=1, source_target_pairs={{1,0},{2,1},{3,2},{5,4},{6,5},{7,6},{9,8},{10,9},{11,10},{13,12},{... | collective-permute-start | bytes 319496 | tf_op jit(solution)/shard_map/ppermute | solution.py:367
  20.6 0.0 collective-permute-done.2.left
  20.6 0.0 copy-start.2
  20.6 3.2 %collective-permute-done.3.right = f32[16,1664]{1,0:T(8,128)S(1)} collective-permute-done((f32[16,1664]{1,0:T(8,128)}, f32[16,1664]{1,0:T(8,128)S(1)}, u32[]{:S(2)}, u32[]{:S(2)}) %collective-permute-start.3) | collective-permute-done | bytes 106528 | tf_op jit(solution)/shard_map/ppermute | solution.py:367
  23.8 0.0 copy-done
  23.8 0.0 copy-done.1
  23.8 0.0 copy-done.2
  23.8 0.0 copy-start.3
  23.8 0.6 copy-done.3
  24.5 60.2 %starlet.1 = (f32[1536,3072]{1,0:T(8,128)}, f32[1536,3072]{1,0:T(8,128)}, f32[1536,3072]{1,0:T(8,128)}, f32[1536,3072]{1,0:T(8,128)}, f32[32,1,128]{2,1,0:T(1,128)}) custom-call(f32[1536,3072]{1,0:T(8,128)} %bitcast.17, f32[16,3072]{1,0:T(8,128)} %copy-done.1, f32[16,3072]{1,0:T(8,128)} %copy-done, f32[16,1664]{1,0:T(8,128)} %copy-done.2, ...), custom_call_target="tpu_custom_call" | custom-call | tf_op jit(solution)/shard_map/starlet/pallas_call | solution.py:321
  84.7 14.9 %all_to_all.5 = f32[32,1,128]{2,1,0:T(1,128)S(1)} all-to-all(f32[32,1,128]{2,1,0:T(1,128)} %get-tuple-element.18), channel_id=1, replica_groups=mesh['rows'=8,'cols'=4] {'rows','cols'}, dimensions={0} | all-to-all | bytes 32768 | tf_op jit(solution)/shard_map/all_to_all | solution.py:385
  99.6 0.1 reduce_sum.9
  99.6 0.5 sqrt_bitcast_fusion
Async XLA Ops:
  1.7 9.8 %collective-permute-start.1 = (f32[16,3072]{1,0:T(8,128)S(1)}, f32[16,3072]{1,0:T(8,128)S(1)}, u32[]{:S(2)}, u32[]{:S(2)}) collective-permute-start(f32[16,3072]{1,0:T(8,128)S(1)} %get-tuple-element.19), channel_id=1, source_target_pairs={{4,0},{8,4},{12,8},{16,12},{20,16},{24,20},{28,24},{5,1},{9,5},{13... | collective-permute-start | bytes 589832 | tf_op jit(solution)/shard_map/ppermute | solution.py:367
  3.0 12.8 %collective-permute-start = (f32[16,3072]{1,0:T(8,128)S(1)}, f32[16,3072]{1,0:T(8,128)S(1)}, u32[]{:S(2)}, u32[]{:S(2)}) collective-permute-start(f32[16,3072]{1,0:T(8,128)S(1)} %get-tuple-element.20), channel_id=1, source_target_pairs={{0,4},{4,8},{8,12},{12,16},{16,20},{20,24},{24,28},{1,5},{5,9},{9,... | collective-permute-start | bytes 589832 | tf_op jit(solution)/shard_map/ppermute | solution.py:367
  11.5 12.4 %copy-start = (f32[16,3072]{1,0:T(8,128)}, f32[16,3072]{1,0:T(8,128)S(1)}, u32[]{:S(2)}) copy-start(f32[16,3072]{1,0:T(8,128)S(1)} %collective-permute-done.1.bottom) | copy-start | bytes 589828
  15.8 8.0 %copy-start.1 = (f32[16,3072]{1,0:T(8,128)}, f32[16,3072]{1,0:T(8,128)S(1)}, u32[]{:S(2)}) copy-start(f32[16,3072]{1,0:T(8,128)S(1)} %collective-permute-done.top) | copy-start | bytes 589828
  16.7 3.9 %collective-permute-start.2 = (f32[16,1664]{1,0:T(8,128)}, f32[16,1664]{1,0:T(8,128)S(1)}, u32[]{:S(2)}, u32[]{:S(2)}) collective-permute-start(f32[16,1664]{1,0:T(8,128)} %fusion.1.last), channel_id=1, source_target_pairs={{0,1},{1,2},{2,3},{4,5},{5,6},{6,7},{8,9},{9,10},{10,11},{12,13},{... | collective-permute-start | bytes 319496 | tf_op jit(solution)/shard_map/ppermute | solution.py:367
  19.3 4.5 %collective-permute-start.3 = (f32[16,1664]{1,0:T(8,128)}, f32[16,1664]{1,0:T(8,128)S(1)}, u32[]{:S(2)}, u32[]{:S(2)}) collective-permute-start(f32[16,1664]{1,0:T(8,128)} %fusion.first), channel_id=1, source_target_pairs={{1,0},{2,1},{3,2},{5,4},{6,5},{7,6},{9,8},{10,9},{11,10},{13,12},{... | collective-permute-start | bytes 319496 | tf_op jit(solution)/shard_map/ppermute | solution.py:367
  20.6 3.2 %copy-start.2 = (f32[16,1664]{1,0:T(8,128)}, f32[16,1664]{1,0:T(8,128)S(1)}, u32[]{:S(2)}) copy-start(f32[16,1664]{1,0:T(8,128)S(1)} %collective-permute-done.2.left) | copy-start | bytes 319492
  23.8 0.6 copy-start.3

commit v4 on v3

--- a/solution.py
+++ b/solution.py
@@ -256,10 +256,10 @@
 
                 def inner(r, c, names=names):
                     m, ml = c
-                    for name in reversed(names):
-                        at = Place(name, p, r, m, ml)
-                        for u in (0, 1):
-                            stages[name](at, u)
+                    places = {name: Place(name, p, r, m, ml) for name in names}
+                    for u in (0, 1):
+                        for name in reversed(names):
+                            stages[name](places[name], u)
                     m, ml = m + 2, ml + 2
                     return jnp.where(m >= ring, m - ring, m), jnp.where(ml >= long, ml - long, ml)
 

time: 100 us -> 101 us (1.010)
  no operation moved by 1% of the time
where the time goes in v4:
time: 101 us; the launch traced here: 100 us
  Pallas kernels  62.8 us (62%)
  blocking collectives  14.9 us (15%)
  starting transfers between devices  10 us (10%)
  waiting for transfers between devices  7.8 us (8%)
  local copies, waits for them, and re-layouts  2.12 us (2%)
  other arithmetic  1.92 us (2%)
    pallas_call x1, Pallas kernels, transform(): pl.pallas_call(functools.partial(kernel, rows=rows, strips=strips), in_sp...  60.3 us
    all_to_all x1, blocking collectives, on_device(): sums = jnp.sum(lax.all_to_all(squares, ('rows', 'cols'), 0, 0), axis=(0, 1))  14.9 us
    ppermute x4, starting transfers between devices, neighbours(): return (lax.ppermute(last, axis, up), lax.ppermute(first, axis, down))  10 us
    ppermute x4, waiting for transfers between devices, neighbours(): return (lax.ppermute(last, axis, up), lax.ppermute(first, axis, down))  7.8 us
    pallas_call x1, Pallas kernels, turned_edges(): pl.pallas_call(edge_kernel, grid=(1,), in_specs=[strip(0), strip(cols //...  2.52 us
  transfers between devices with their start and end apart: 4, of which 3 were waited for; matrix products, arithmetic and copies ran while one was open for 1% of the time, Pallas kernels for 3%

profile of v4, /device:TPU:0, one launch (start us, length us, event | category | flops | bytes accessed | tf_op | source)
XLA Modules:
  0.0 100.2 jit_solution(4852132482165651691)
XLA Ops:
  0.6 1.1 %slice_bitcast_fusion = (f32[16,3072]{1,0:T(8,128)S(1)}, f32[16,3072]{1,0:T(8,128)S(1)}) fusion(f32[1,1536,3072]{2,1,0:T(8,128)} %param.1), kind=kLoop, calls=%fused_computation | loop fusion | bytes 786432 | tf_op jit(solution)/shard_map/slice | solution.py:375
  1.7 1.3 %collective-permute-start.1 = (f32[16,3072]{1,0:T(8,128)S(1)}, f32[16,3072]{1,0:T(8,128)S(1)}, u32[]{:S(2)}, u32[]{:S(2)}) collective-permute-start(f32[16,3072]{1,0:T(8,128)S(1)} %get-tuple-element.19), channel_id=1, source_target_pairs={{4,0},{8,4},{12,8},{16,12},{20,16},{24,20},{28,24},{5,1},{9,5},{13... | collective-permute-start | bytes 589832 | tf_op jit(solution)/shard_map/ppermute | solution.py:367
  3.0 5.5 %collective-permute-start = (f32[16,3072]{1,0:T(8,128)S(1)}, f32[16,3072]{1,0:T(8,128)S(1)}, u32[]{:S(2)}, u32[]{:S(2)}) collective-permute-start(f32[16,3072]{1,0:T(8,128)S(1)} %get-tuple-element.20), channel_id=1, source_target_pairs={{0,4},{4,8},{8,12},{12,16},{16,20},{20,24},{24,28},{1,5},{5,9},{9,... | collective-permute-start | bytes 589832 | tf_op jit(solution)/shard_map/ppermute | solution.py:367
  8.5 2.5 %edges.1 = (f32[16,1664]{1,0:T(8,128)}, f32[16,1664]{1,0:T(8,128)}) custom-call(f32[1536,3072]{1,0:T(8,128)} %bitcast.15, f32[1536,3072]{1,0:T(8,128)} %bitcast.16), custom_call_target="tpu_custom_call" | custom-call | bytes 1572864 | tf_op jit(solution)/shard_map/edges/pallas_call | solution.py:352
  11.0 0.4 collective-permute-done.1.bottom
  11.5 0.0 copy-start
  11.5 0.1 fusion.3
  11.5 0.1 copy.17
  11.6 0.1 copy.15
  11.7 4.1 %collective-permute-done.top = f32[16,3072]{1,0:T(8,128)S(1)} collective-permute-done((f32[16,3072]{1,0:T(8,128)S(1)}, f32[16,3072]{1,0:T(8,128)S(1)}, u32[]{:S(2)}, u32[]{:S(2)}) %collective-permute-start) | collective-permute-done | bytes 196640 | tf_op jit(solution)/shard_map/ppermute | solution.py:367
  15.8 0.0 copy-start.1
  15.8 0.1 fusion.2
  15.9 0.1 copy.16
  16.0 0.1 copy.14
  16.0 0.7 fusion.1.last
  16.7 1.9 %collective-permute-start.2 = (f32[16,1664]{1,0:T(8,128)}, f32[16,1664]{1,0:T(8,128)S(1)}, u32[]{:S(2)}, u32[]{:S(2)}) collective-permute-start(f32[16,1664]{1,0:T(8,128)} %fusion.1.last), channel_id=1, source_target_pairs={{0,1},{1,2},{2,3},{4,5},{5,6},{6,7},{8,9},{9,10},{10,11},{12,13},{... | collective-permute-start | bytes 319496 | tf_op jit(solution)/shard_map/ppermute | solution.py:367
  18.6 0.7 fusion.first
  19.3 1.3 %collective-permute-start.3 = (f32[16,1664]{1,0:T(8,128)}, f32[16,1664]{1,0:T(8,128)S(1)}, u32[]{:S(2)}, u32[]{:S(2)}) collective-permute-start(f32[16,1664]{1,0:T(8,128)} %fusion.first), channel_id=1, source_target_pairs={{1,0},{2,1},{3,2},{5,4},{6,5},{7,6},{9,8},{10,9},{11,10},{13,12},{... | collective-permute-start | bytes 319496 | tf_op jit(solution)/shard_map/ppermute | solution.py:367
  20.6 0.0 collective-permute-done.2.left
  20.6 0.0 copy-start.2
  20.6 3.2 %collective-permute-done.3.right = f32[16,1664]{1,0:T(8,128)S(1)} collective-permute-done((f32[16,1664]{1,0:T(8,128)}, f32[16,1664]{1,0:T(8,128)S(1)}, u32[]{:S(2)}, u32[]{:S(2)}) %collective-permute-start.3) | collective-permute-done | bytes 106528 | tf_op jit(solution)/shard_map/ppermute | solution.py:367
  23.8 0.0 copy-done
  23.8 0.0 copy-done.1
  23.8 0.0 copy-done.2
  23.8 0.0 copy-start.3
  23.8 0.6 copy-done.3
  24.5 60.3 %starlet.1 = (f32[1536,3072]{1,0:T(8,128)}, f32[1536,3072]{1,0:T(8,128)}, f32[1536,3072]{1,0:T(8,128)}, f32[1536,3072]{1,0:T(8,128)}, f32[32,1,128]{2,1,0:T(1,128)}) custom-call(f32[1536,3072]{1,0:T(8,128)} %bitcast.17, f32[16,3072]{1,0:T(8,128)} %copy-done.1, f32[16,3072]{1,0:T(8,128)} %copy-done, f32[16,1664]{1,0:T(8,128)} %copy-done.2, ...), custom_call_target="tpu_custom_call" | custom-call | tf_op jit(solution)/shard_map/starlet/pallas_call | solution.py:321
  84.8 14.9 %all_to_all.5 = f32[32,1,128]{2,1,0:T(1,128)S(1)} all-to-all(f32[32,1,128]{2,1,0:T(1,128)} %get-tuple-element.18), channel_id=1, replica_groups=mesh['rows'=8,'cols'=4] {'rows','cols'}, dimensions={0} | all-to-all | bytes 32768 | tf_op jit(solution)/shard_map/all_to_all | solution.py:385
  99.7 0.1 reduce_sum.9
  99.7 0.5 sqrt_bitcast_fusion
Async XLA Ops:
  1.7 9.8 %collective-permute-start.1 = (f32[16,3072]{1,0:T(8,128)S(1)}, f32[16,3072]{1,0:T(8,128)S(1)}, u32[]{:S(2)}, u32[]{:S(2)}) collective-permute-start(f32[16,3072]{1,0:T(8,128)S(1)} %get-tuple-element.19), channel_id=1, source_target_pairs={{4,0},{8,4},{12,8},{16,12},{20,16},{24,20},{28,24},{5,1},{9,5},{13... | collective-permute-start | bytes 589832 | tf_op jit(solution)/shard_map/ppermute | solution.py:367
  3.0 12.8 %collective-permute-start = (f32[16,3072]{1,0:T(8,128)S(1)}, f32[16,3072]{1,0:T(8,128)S(1)}, u32[]{:S(2)}, u32[]{:S(2)}) collective-permute-start(f32[16,3072]{1,0:T(8,128)S(1)} %get-tuple-element.20), channel_id=1, source_target_pairs={{0,4},{4,8},{8,12},{12,16},{16,20},{20,24},{24,28},{1,5},{5,9},{9,... | collective-permute-start | bytes 589832 | tf_op jit(solution)/shard_map/ppermute | solution.py:367
  11.5 12.4 %copy-start = (f32[16,3072]{1,0:T(8,128)}, f32[16,3072]{1,0:T(8,128)S(1)}, u32[]{:S(2)}) copy-start(f32[16,3072]{1,0:T(8,128)S(1)} %collective-permute-done.1.bottom) | copy-start | bytes 589828
  15.8 8.0 %copy-start.1 = (f32[16,3072]{1,0:T(8,128)}, f32[16,3072]{1,0:T(8,128)S(1)}, u32[]{:S(2)}) copy-start(f32[16,3072]{1,0:T(8,128)S(1)} %collective-permute-done.top) | copy-start | bytes 589828
  16.7 3.9 %collective-permute-start.2 = (f32[16,1664]{1,0:T(8,128)}, f32[16,1664]{1,0:T(8,128)S(1)}, u32[]{:S(2)}, u32[]{:S(2)}) collective-permute-start(f32[16,1664]{1,0:T(8,128)} %fusion.1.last), channel_id=1, source_target_pairs={{0,1},{1,2},{2,3},{4,5},{5,6},{6,7},{8,9},{9,10},{10,11},{12,13},{... | collective-permute-start | bytes 319496 | tf_op jit(solution)/shard_map/ppermute | solution.py:367
  19.3 4.5 %collective-permute-start.3 = (f32[16,1664]{1,0:T(8,128)}, f32[16,1664]{1,0:T(8,128)S(1)}, u32[]{:S(2)}, u32[]{:S(2)}) collective-permute-start(f32[16,1664]{1,0:T(8,128)} %fusion.first), channel_id=1, source_target_pairs={{1,0},{2,1},{3,2},{5,4},{6,5},{7,6},{9,8},{10,9},{11,10},{13,12},{... | collective-permute-start | bytes 319496 | tf_op jit(solution)/shard_map/ppermute | solution.py:367
  20.6 3.2 %copy-start.2 = (f32[16,1664]{1,0:T(8,128)}, f32[16,1664]{1,0:T(8,128)S(1)}, u32[]{:S(2)}) copy-start(f32[16,1664]{1,0:T(8,128)S(1)} %collective-permute-done.2.left) | copy-start | bytes 319492
  23.8 0.6 copy-start.3
